TPU v7x, 32 devices: a whole 2x2x4 slice. The times are simulated.
32 devices in a mesh: dp: 16 (over z, y, x), rep: 2 (over core).
Axes of the slice: x: 2, y: 2, z: 4, core: 2. Of those that a mesh axis runs over, the one named last changes fastest.
Arguments:
- images: bfloat16 [1024, 145, 768], P(('dp', 'rep')), may hold values from -6 to 6
- groups: int32 [1024], P(('dp', 'rep')), may hold values from 0 to 1, as said below
- captions: bfloat16 [1024, 16, 768], P(('dp', 'rep')), may hold values from -6 to 6
- cap_lengths: int32 [1024], P(('dp', 'rep')), may hold values from 4 to 16, as said below
- img_gain_a: bfloat16 [768], P('rep'), may hold values from 0.5 to 1.5
- img_w_qkv: bfloat16 [768, 2304], P('rep'), may hold values from -0.21875 to 0.21875
- img_b_qv: bfloat16 [1536], P('rep'), may hold values from -3 to 3
- img_w_out: bfloat16 [768, 768], P('rep'), may hold values from -0.625 to 0.625
- img_gain_m: bfloat16 [768], P('rep'), may hold values from 0.5 to 1.5
- img_w_up: bfloat16 [768, 3072], P('rep'), may hold values from -0.21875 to 0.21875
- img_b_up: bfloat16 [3072], P('rep'), may hold values from -3 to 3
- img_w_down: bfloat16 [3072, 768], P('rep'), may hold values from -0.109375 to 0.109375
- gain_attn: bfloat16 [768], replicated, may hold values from 0.5 to 1.5
- w_qkv: bfloat16 [768, 2304], replicated, may hold values from -0.21875 to 0.21875
- b_qv: bfloat16 [1536], replicated, may hold values from -3 to 3
- w_out: bfloat16 [768, 768], replicated, may hold values from -0.625 to 0.625
- gain_mlp: bfloat16 [768], replicated, may hold values from 0.5 to 1.5
- w_up: bfloat16 [768, 3072], replicated, may hold values from -0.21875 to 0.21875
- b_up: bfloat16 [3072], replicated, may hold values from -3 to 3
- w_down: bfloat16 [3072, 768], replicated, may hold values from -0.109375 to 0.109375
- text_proj: bfloat16 [768, 768], replicated, may hold values from -0.21875 to 0.21875
Outputs:
- pair_loss: float32 [1024], P(('dp', 'rep'))
- caption_grad: float32 [1024, 16, 768], P(('dp', 'rep'))
- grad_gain_attn: float32 [768], P('rep')
- grad_w_qkv: float32 [768, 2304], P(None, 'rep')
- grad_b_qv: float32 [1536], P('rep')
- grad_w_out: float32 [768, 768], P(None, 'rep')
- grad_gain_mlp: float32 [768], P('rep')
- grad_w_up: float32 [768, 3072], P(None, 'rep')
- grad_b_up: float32 [3072], P('rep')
- grad_w_down: float32 [3072, 768], P(None, 'rep')
Inputs may be any that keep to these rules, and one draw needn't show every extreme that they name: `groups`: 1 marks an image of 145 tokens, 0 one of 50 tokens whose later positions are unused; the 32 pairs of every device hold images of both kinds. Positions of a caption from cap_lengths on are padding; the 32 pairs of every device hold a caption of 16 tokens.
All inputs are finite; a program needn't handle non-finite values.
Results may differ from a plain program's by a relative error of at most 0.0165.
Values may be sent and summed in bfloat16 or wider, within the bound.
No kernel may reach another device: no remote copies, remote signals or barrier semaphores. Data moves between devices by JAX's collectives and lax.ppermute only.
A program may use at most 192 MiB of HBM per device.

v0:
```python
import functools
import math

import jax
import jax.numpy as jnp
from jax import lax
from jax.experimental import pallas as pl
from jax.experimental.pallas import tpu as pltpu
from jax.sharding import PartitionSpec as P

D = 768
HEADS = 12
FF = 3072
ILEN = 145
LOWLEN = 50
CAP = 16

SCALE = 100.0
EPS = 1e-06
NEGATIVE = -1e30
LOG2E = math.log2(math.e)
MOST_PAIRS = 2048

UNIT = 160
UNITS = 2
PART = 48
SPAN = 29
QB = 128
BW = 3 * D // 2 + D // 2 + 128
EARLY = D + 128
CHUNKS = 16

f32 = jnp.float32
bf16 = jnp.bfloat16


def dot(left_side, right_side):
    return jnp.dot(left_side, right_side, preferred_element_type=f32)


def dot_nt(left_side, right_side):
    return lax.dot_general(
        left_side, right_side, (((1,), (1,)), ((), ())), preferred_element_type=f32
    )


def dot_tn(left_side, right_side):
    return lax.dot_general(
        left_side, right_side, (((0,), (0,)), ((), ())), preferred_element_type=f32
    )


def normalize(values):
    center = values - jnp.mean(values, -1, keepdims=True)
    inverse = lax.rsqrt(jnp.mean(center * center, -1, keepdims=True) + EPS)
    return center * inverse, inverse


def norm_back(grad, normed, inverse):
    return inverse * (
        grad
        - jnp.mean(grad, -1, keepdims=True)
        - normed * jnp.mean(grad * normed, -1, keepdims=True)
    )


def normal_cdf(values):
    return 0.5 + 0.5 * lax.erf(values * (1.0 / math.sqrt(2.0)))


def split_low(values):
    big = values.astype(bf16)
    return big, (values - big.astype(f32)).astype(bf16)


def tower_kernel(
    groups_ref,
    mine_ref,
    x_hbm,
    vec_own_ref,
    vec_other_ref,
    qkv_own,
    qkv_other,
    out_own,
    out_other,
    up_own,
    up_other,
    down_own,
    down_other,
    emb_ref,
    order,
    x_ref,
    x_wide,
    wqkv,
    wout,
    wup,
    wdown,
    gain_a,
    bqkv,
    gain_m,
    bup,
    xs,
    qkv,
    mixed,
    asum,
    hsum,
    aparts,
    hparts,
    scores,
    attention,
    sems,
):
    total = x_ref.shape[1]
    pitch = total + 8
    mine = mine_ref[0]
    copies = []
    for k in range(ILEN // SPAN):
        span = pl.ds(k * SPAN, SPAN)
        copies.append(pltpu.make_async_copy(x_hbm.at[span], x_ref.at[span], sems.at[8 + k]))
    for k, (own, other, whole) in enumerate(
        (
            (qkv_own, qkv_other, wqkv),
            (out_own, out_other, wout),
            (up_own, up_other, wup),
            (down_own, down_other, wdown),
        )
    ):
        half = own.shape[0]
        copies.append(
            pltpu.make_async_copy(own, whole.at[pl.ds(mine * half, half)], sems.at[2 * k])
        )
        copies.append(
            pltpu.make_async_copy(
                other, whole.at[pl.ds((1 - mine) * half, half)], sems.at[2 * k + 1]
            )
        )
    for copy in copies:
        copy.start()

    vec_own = vec_own_ref[...].astype(f32)
    vec_other = vec_other_ref[...].astype(f32)
    low = jnp.where(mine == 0, vec_own, vec_other)
    high = jnp.where(mine == 0, vec_other, vec_own)
    start = 0
    for dest, size, at in (
        (gain_a, D // 2, (0, D // 2)),
        (bqkv, D, (0, 2 * D)),
        (gain_m, D // 2, (0, D // 2)),
        (bup, FF // 2, (0, FF // 2)),
    ):
        dest[:, at[0] : at[0] + size] = low[:, start : start + size]
        dest[:, at[1] : at[1] + size] = high[:, start : start + size]
        start += size
    bqkv[:, D : 2 * D] = jnp.zeros((1, D), f32)

    def count(i, found):
        return found + groups_ref[i]

    n_hi = lax.fori_loop(0, total, count, 0)

    def place_one(i, state):
        hi, lo = state
        group = groups_ref[i]
        order[jnp.where(group == 1, hi, lo)] = i
        return hi + group, lo + 1 - group

    lax.fori_loop(0, total, place_one, (0, n_hi))
    n_units = n_hi + (total - n_hi + 2) // 3

    xs[...] = jnp.zeros_like(xs)
    first = lax.broadcasted_iota(jnp.int32, (1, 128), 1) < 64
    key_at = lax.broadcasted_iota(jnp.int32, (UNIT, UNIT), 1)
    row_at = lax.broadcasted_iota(jnp.int32, (UNIT, UNIT), 0)
    sub = lax.broadcasted_iota(jnp.int32, (8, 1), 0)

    def place(unit, k):
        last = jnp.minimum(unit, n_units - 1)
        is_hi = last < n_hi
        where = jnp.where(is_hi, last, n_hi + 3 * (last - n_hi) + k)
        return order[jnp.minimum(where, total - 1)], is_hi

    def keep_parts(values, j, dest, col, width):
        rows = values.reshape(UNIT // 8, 8, width)
        parts = [
            jnp.sum(rows[0:6], 0),
            rows[6],
            jnp.sum(rows[7:12], 0),
            rows[12],
            jnp.sum(rows[13:18], 0),
            rows[18],
        ]
        for k, part in enumerate(parts):
            dest[j * PART + k * 8 : j * PART + k * 8 + 8, col : col + width] = part

    loads = copies[: ILEN // SPAN]
    copies = copies[ILEN // SPAN :]

    def widen(t, carry):
        for panel in range(D // 128):
            x_wide[panel, pl.ds(pl.multiple_of(t * pitch, 8), total), :] = x_ref[
                t, :, panel * 128 : (panel + 1) * 128
            ].astype(f32)
        return carry

    for k, load in enumerate(loads):
        load.wait()
        lax.fori_loop(k * SPAN, (k + 1) * SPAN, widen, 0)
    for copy in copies[:2]:
        copy.wait()

    def body(step, carry):
        for j in range(UNITS):
            unit = step * UNITS + j
            one, is_hi = place(unit, 0)
            two, three = place(unit, 1)[0], place(unit, 2)[0]
            base = j * UNIT

            @pl.when(is_hi)
            def _():
                for panel in range(D // 128):
                    xs[base : base + ILEN, panel * 128 : (panel + 1) * 128] = x_wide[
                        panel, pl.ds(one, ILEN, stride=pitch), :
                    ]

            @pl.when(jnp.logical_not(is_hi))
            def _():
                for k, index in enumerate((one, two, three)):
                    for panel in range(D // 128):
                        xs[
                            base + LOWLEN * k : base + LOWLEN * (k + 1),
                            panel * 128 : (panel + 1) * 128,
                        ] = x_wide[panel, pl.ds(index, LOWLEN, stride=pitch), :]

        low_rows = (normalize(xs[...])[0] * gain_a[...]).astype(bf16)
        for col in range(0, 3 * D, 256):
            values = dot(low_rows, wqkv[:, col : col + 256]) + bqkv[:, col : col + 256]
            if col < D:
                values = values * (LOG2E / 8.0)
            qkv[:, col : col + 256] = values.astype(bf16)

        @pl.when(step == 0)
        def _():
            for copy in copies[2:6]:
                copy.wait()

        for j in range(UNITS):
            is_hi = place(step * UNITS + j, 0)[1]
            base = j * UNIT
            key_seg = jnp.where(key_at < LOWLEN, 0, jnp.where(key_at < 2 * LOWLEN, 1, 2))
            row_seg = jnp.where(row_at < LOWLEN, 0, jnp.where(row_at < 2 * LOWLEN, 1, 2))
            short_ok = jnp.logical_and(key_seg == row_seg, key_at < 3 * LOWLEN)
            allowed = jnp.where(
                is_hi, (key_at < ILEN).astype(jnp.int32), short_ok.astype(jnp.int32)
            )
            bias = jnp.where(allowed > 0, 0.0, NEGATIVE)
            for p in range(HEADS // 2):
                query = qkv[base : base + UNIT, p * 128 : (p + 1) * 128]
                key = qkv[base : base + UNIT, D + p * 128 : D + (p + 1) * 128]
                for h in range(2):
                    head = first if h == 0 else jnp.logical_not(first)
                    at = (j * HEADS + 2 * p + h) * UNIT
                    scores[at : at + UNIT, :] = (
                        dot_nt(jnp.where(head, query, jnp.zeros_like(query)), key) + bias
                    )
        for j in range(UNITS):
            part = slice(j * HEADS * UNIT, (j + 1) * HEADS * UNIT)
            values = scores[part, :]
            powers = jnp.exp2(values - jnp.max(values, 1, keepdims=True))
            attention[part, :] = powers.astype(bf16)
        for j in range(UNITS):
            base = j * UNIT
            for p in range(HEADS // 2):
                lanes = slice(p * 128, (p + 1) * 128)
                value = qkv[base : base + UNIT, 2 * D + p * 128 : 2 * D + (p + 1) * 128]
                outs = []
                at = (j * HEADS + 2 * p) * UNIT
                value_one = jnp.concatenate([value, jnp.ones_like(value)], 1)
                for h in range(2):
                    summed = dot(attention[at + h * UNIT : at + (h + 1) * UNIT, :], value_one)
                    outs.append(summed[:, :128] / summed[:, 128:])
                mixed[base : base + UNIT, lanes] = jnp.where(first, outs[0], outs[1]).astype(bf16)
        for col in range(0, D, 256):
            xs[:, col : col + 256] += dot(mixed[...], wout[:, col : col + 256])
        for j in range(UNITS):
            keep_parts(xs[j * UNIT : (j + 1) * UNIT, :], j, aparts, 0, D)
        low_two = (normalize(xs[...])[0] * gain_m[...]).astype(bf16)
        width = 1024
        for col in range(0, FF, width):
            pre_act = dot(low_two, wup[:, col : col + width]) + bup[:, col : col + width]
            hidden = pre_act * normal_cdf(pre_act)
            for j in range(UNITS):
                keep_parts(hidden[j * UNIT : (j + 1) * UNIT], j, hparts, col, width)
        for j in range(UNITS):
            unit = step * UNITS + j
            one, is_hi = place(unit, 0)
            two, three = place(unit, 1)[0], place(unit, 2)[0]

            def rows_of(index):
                return pl.ds(pl.multiple_of(index * 8, 8), 8)

            @pl.when(is_hi)
            def _():
                for src, dest in ((aparts, asum), (hparts, hsum)):
                    part = [src[j * PART + k * 8 : j * PART + k * 8 + 8, :] for k in range(6)]
                    dest[rows_of(one), :] = (
                        (part[0] + part[1])
                        + (part[2] + part[3])
                        + (part[4] + jnp.where(sub < 1, part[5], 0.0))
                    )

            @pl.when(jnp.logical_not(is_hi))
            def _():
                for src, dest in ((aparts, asum), (hparts, hsum)):
                    part = [src[j * PART + k * 8 : j * PART + k * 8 + 8, :] for k in range(6)]
                    dest[rows_of(three), :] = (
                        jnp.where(sub < 4, 0.0, part[3])
                        + part[4]
                        + jnp.where(sub < 6, part[5], 0.0)
                    )
                    dest[rows_of(two), :] = (
                        jnp.where(sub < 2, 0.0, part[1])
                        + part[2]
                        + jnp.where(sub < 4, part[3], 0.0)
                    )
                    dest[rows_of(one), :] = part[0] + jnp.where(sub < 2, part[1], 0.0)

        return carry

    lax.fori_loop(0, (n_units + UNITS - 1) // UNITS, body, 0)
    for copy in copies[6:]:
        copy.wait()
    which = lax.broadcasted_iota(jnp.int32, (total, 128), 0)
    scale = jnp.zeros((total, 128), f32)
    for i in range(total):
        scale = jnp.where(
            which == i, jnp.where(groups_ref[i] == 1, 1.0 / ILEN, 1.0 / LOWLEN), scale
        )
    scale = scale[:, 0:1]
    big, rest = split_low(jnp.sum(hsum[...].reshape(total, 8, FF), 1) * scale)
    product = dot(jnp.concatenate([big, rest], 0), wdown[...])
    pooled = jnp.sum(asum[...].reshape(total, 8, D), 1) * scale + product[:total] + product[total:]
    emb_ref[...] = (
        pooled * lax.rsqrt(jnp.sum(pooled * pooled, -1, keepdims=True) + EPS)
    ).astype(bf16)


VM = pl.BlockSpec(memory_space=pltpu.VMEM)
SM = pl.BlockSpec(memory_space=pltpu.SMEM)
ANY = pl.BlockSpec(memory_space=pltpu.HBM)


def limit(mebibytes):
    return pltpu.CompilerParams(vmem_limit_bytes=mebibytes * 1024 * 1024)


def image_tower(images, groups, mine, vec_own, vec_other, weights):
    number = images.shape[1]
    rows = UNITS * UNIT
    flops = number * 100 * 2 * (4 * D * D + D * FF)
    return pl.pallas_call(
        tower_kernel,
        out_shape=jax.ShapeDtypeStruct((number, D), bf16),
        in_specs=[SM, SM, ANY, VM, VM] + [ANY] * 8,
        out_specs=VM,
        scratch_shapes=[
            pltpu.SMEM((number,), jnp.int32),
            pltpu.VMEM(images.shape, bf16),
            pltpu.VMEM((D // 128, ILEN * (number + 8), 128), f32),
            pltpu.VMEM((D, 3 * D), bf16),
            pltpu.VMEM((D, D), bf16),
            pltpu.VMEM((D, FF), bf16),
            pltpu.VMEM((FF, D), bf16),
            pltpu.VMEM((1, D), f32),
            pltpu.VMEM((1, 3 * D), f32),
            pltpu.VMEM((1, D), f32),
            pltpu.VMEM((1, FF), f32),
            pltpu.VMEM((rows, D), f32),
            pltpu.VMEM((rows, 3 * D), bf16),
            pltpu.VMEM((rows, D), bf16),
            pltpu.VMEM((number * 8, D), f32),
            pltpu.VMEM((number * 8, FF), f32),
            pltpu.VMEM((UNITS * PART, D), f32),
            pltpu.VMEM((UNITS * PART, FF), f32),
            pltpu.VMEM((UNITS * HEADS * UNIT, UNIT), f32),
            pltpu.VMEM((UNITS * HEADS * UNIT, UNIT), bf16),
            pltpu.SemaphoreType.DMA((8 + ILEN // SPAN,)),
        ],
        compiler_params=limit(62),
        cost_estimate=pl.CostEstimate(
            flops=flops, bytes_accessed=24 * 1024 * 1024, transcendentals=0
        ),
        name="image_tower",
    )(groups, mine, images, vec_own, vec_other, *weights)


def lens_along(lens_ref, start, number):
    owner = lax.broadcasted_iota(jnp.int32, (1, number * CAP), 1) // CAP
    lens = jnp.zeros((1, number * CAP), jnp.int32)
    for c in range(number):
        lens = jnp.where(owner == c, lens_ref[start + c], lens)
    return lens


def score_bias(lens_ref, block):
    per = QB // CAP
    position = lax.broadcasted_iota(jnp.int32, (1, QB), 1) % CAP
    valid = position < lens_along(lens_ref, block * per, per)
    rows = lax.broadcasted_iota(jnp.int32, (QB, QB), 0) // CAP
    columns = lax.broadcasted_iota(jnp.int32, (QB, QB), 1) // CAP
    return jnp.where(jnp.logical_and(rows == columns, valid), 0.0, NEGATIVE)


def forward_kernel(
    lens_ref,
    x_ref,
    vec_ref,
    wqkv_ref,
    wout_ref,
    wup_ref,
    wdown_ref,
    qkv,
    mixed,
    after,
    mlp,
    slope,
    attention,
    early,
    hidden,
    scores,
):
    rows = x_ref.shape[0]
    number = rows // CAP
    first = lax.broadcasted_iota(jnp.int32, (1, 128), 1) < 64
    normed, _ = normalize(x_ref[...].astype(f32))
    low = (normed * vec_ref[:, 0:D]).astype(bf16)
    for col in range(0, 3 * D, 256):
        values = dot(low, wqkv_ref[:, col : col + 256])
        if col < D:
            values = values + vec_ref[:, D + col : D + col + 256]
        if col >= 2 * D:
            values = values + vec_ref[:, col : col + 256]
        values = values.astype(bf16)
        if col < D:
            values = values * jnp.asarray(0.125, bf16)
        qkv[:, col : col + 256] = values
    for block in range(rows // QB):
        bias = score_bias(lens_ref, block)
        span = slice(block * QB, (block + 1) * QB)
        for p in range(HEADS // 2):
            query = qkv[span, p * 128 : (p + 1) * 128]
            key = qkv[span, D + p * 128 : D + (p + 1) * 128]
            for h in range(2):
                head = first if h == 0 else jnp.logical_not(first)
                at = (block * HEADS + 2 * p + h) * QB
                scores[at : at + QB, :] = (
                    dot_nt(jnp.where(head, query, jnp.zeros_like(query)), key) * LOG2E + bias
                )
    for block in range(rows // QB):
        part = slice(block * HEADS * QB, (block + 1) * HEADS * QB)
        values = scores[part, :]
        powers = jnp.exp2(values - jnp.max(values, 1, keepdims=True))
        attention[part, :] = (powers * (1.0 / jnp.sum(powers, 1, keepdims=True))).astype(bf16)
    for block in range(rows // QB):
        span = slice(block * QB, (block + 1) * QB)
        for p in range(HEADS // 2):
            value = qkv[span, 2 * D + p * 128 : 2 * D + (p + 1) * 128]
            at = (block * HEADS + 2 * p) * QB
            outs = [dot(attention[at + h * QB : at + (h + 1) * QB, :], value) for h in range(2)]
            mixed[span, p * 128 : (p + 1) * 128] = jnp.where(first, outs[0], outs[1]).astype(bf16)
    for col in range(0, D, 256):
        after[:, col : col + 256] = x_ref[:, col : col + 256].astype(f32) + dot(
            mixed[...], wout_ref[:, col : col + 256]
        )
    mlp[...] = (normalize(after[...])[0] * vec_ref[:, 3 * D : 4 * D]).astype(bf16)
    lens = lens_along(lens_ref, 0, number)
    position = lax.broadcasted_iota(jnp.int32, (1, rows), 1)
    owner = (
        lax.broadcasted_iota(jnp.int32, (number, rows), 0)
        == lax.broadcasted_iota(jnp.int32, (number, rows), 1) // CAP
    )
    members = jnp.where(jnp.logical_and(owner, position % CAP < lens), 1.0, 0.0)
    pool = members.astype(bf16)
    count = jnp.sum(members, 1, keepdims=True)
    width = 512
    for col in range(0, FF, width):
        span = slice(col, col + width)
        pre_act = dot(mlp[...], wup_ref[:, span]) + vec_ref[:, 4 * D + col : 4 * D + col + width]
        phi = normal_cdf(pre_act)
        hidden[:, span] = (pre_act * phi).astype(bf16)
        density = jnp.exp2(pre_act * pre_act * (-0.5 * LOG2E)) * (1.0 / math.sqrt(2.0 * math.pi))
        slope[:, span] = (phi + pre_act * density).astype(bf16)
    big, rest = split_low(dot(pool, hidden[...]))
    after_big, after_rest = split_low(after[...])
    pooled = (
        dot(pool, after_big)
        + dot(pool, after_rest)
        + dot(big, wdown_ref[...])
        + dot(rest, wdown_ref[...])
    )
    early[:, 0:D] = (pooled / count).astype(bf16)
    early[:, D:EARLY] = jnp.broadcast_to(count, (number, EARLY - D)).astype(bf16)
    early[:, EARLY:] = big


def text_forward(captions, lens, vec, w_qkv, w_out, w_up, w_down):
    rows = captions.shape[0]
    shape = jax.ShapeDtypeStruct
    return pl.pallas_call(
        forward_kernel,
        out_shape=[
            shape((rows, 3 * D), bf16),
            shape((rows, D), bf16),
            shape((rows, D), f32),
            shape((rows, D), bf16),
            shape((rows, FF), bf16),
            shape((rows * HEADS, QB), bf16),
            shape((rows // CAP, EARLY + FF), bf16),
        ],
        in_specs=[SM] + [VM] * 6,
        out_specs=[VM] * 7,
        scratch_shapes=[pltpu.VMEM((rows, FF), bf16), pltpu.VMEM((rows * HEADS, QB), f32)],
        compiler_params=limit(60),
        cost_estimate=pl.CostEstimate(
            flops=2 * rows * (4 * D * D + 2 * D * FF),
            bytes_accessed=24 * 1024 * 1024,
            transcendentals=0,
        ),
        name="text_forward",
    )(lens, captions, vec, w_qkv, w_out, w_up, w_down)


def put_chunks(dest, values, place_ref, stream, col):
    rows = values.shape[0] // CHUNKS
    for chunk in range(CHUNKS):
        at = pl.multiple_of(place_ref[stream, chunk] * rows, 16)
        dest[pl.ds(at, rows), col : col + values.shape[1]] = values[
            chunk * rows : (chunk + 1) * rows
        ].astype(dest.dtype)


def up_kernel(
    place_ref, mine_ref, lens_ref, branch_ref, slope_ref, mlp_ref, wdown_ref,
    grad_pre, own, other, grad_bup, grad_hidden, mlp_t,
):
    number = slope_ref.shape[0] // CAP
    half = FF // 2
    mine = mine_ref[0]
    for col in range(0, FF, 512):
        grad_hidden[:, col : col + 512] = dot_nt(branch_ref[...], wdown_ref[col : col + 512, :])
    position = lax.broadcasted_iota(jnp.int32, (CAP, 1), 0)
    for c in range(number):
        span = slice(c * CAP, (c + 1) * CAP)
        keep = jnp.where(position < lens_ref[c], 1.0, 0.0)
        grad_pre[span, :] = (
            grad_hidden[c : c + 1, :] * slope_ref[span, :].astype(f32) * keep
        ).astype(bf16)
    mlp_t[...] = mlp_ref[...].T
    for which, dest in ((1 - mine, other), (mine, own)):
        for col in range(0, half, 384):
            lanes = pl.ds(pl.multiple_of(which * half + col, 128), 384)
            put_chunks(dest, dot(mlp_t[...], grad_pre[:, lanes]), place_ref, 2 * col // half, col)
    for col in range(0, FF, 512):
        grad_bup[:, col : col + 512] = jnp.sum(
            grad_pre[:, col : col + 512].astype(f32), 0, keepdims=True
        )


def up_backward(place, mine, lens, branch, slope, mlp, w_down):
    rows = slope.shape[0]
    shape = jax.ShapeDtypeStruct
    return pl.pallas_call(
        up_kernel,
        out_shape=[
            shape((rows, FF), bf16),
            shape((D, FF // 2), f32),
            shape((D, FF // 2), bf16),
            shape((1, FF), f32),
        ],
        in_specs=[SM, SM, SM] + [VM] * 4,
        out_specs=[VM] * 4,
        scratch_shapes=[pltpu.VMEM((rows // CAP, FF), f32), pltpu.VMEM((D, rows), bf16)],
        compiler_params=limit(24),
        cost_estimate=pl.CostEstimate(
            flops=2 * rows * D * FF, bytes_accessed=20 * 1024 * 1024, transcendentals=0
        ),
        name="up_backward",
    )(place, mine, lens, branch, slope, mlp, w_down)


def mlp_kernel(
    lens_ref, pre_ref, grad_ref, after_ref, vec_ref, wup_ref, wout_ref,
    grad_after, grad_mixed, grad_gain, grad_out,
):
    number = after_ref.shape[0] // CAP
    grad_mlp = dot_nt(pre_ref[...], wup_ref[...])
    normed_two, inverse_two = normalize(after_ref[...])
    grad_gain[...] = jnp.sum(grad_mlp * normed_two, 0, keepdims=True)
    grad_after[...] = norm_back(grad_mlp * vec_ref[:, 3 * D : 4 * D], normed_two, inverse_two)
    position = lax.broadcasted_iota(jnp.int32, (CAP, 1), 0)
    for c in range(number):
        keep = jnp.where(position < lens_ref[c], 1.0, 0.0)
        grad_after[c * CAP : (c + 1) * CAP, :] += grad_ref[c : c + 1, :] * keep
    grad_out[...] = grad_after[...].astype(bf16)
    for col in range(0, D, 256):
        grad_mixed[:, col : col + 256] = dot_nt(
            grad_out[...], wout_ref[col : col + 256, :]
        ).astype(bf16)


def mlp_backward(lens, grad_pre, grads, after, vec, w_up, w_out):
    rows = after.shape[0]
    shape = jax.ShapeDtypeStruct
    return pl.pallas_call(
        mlp_kernel,
        out_shape=[shape((rows, D), f32), shape((rows, D), bf16), shape((1, D), f32)],
        in_specs=[SM] + [VM] * 6,
        out_specs=[VM] * 3,
        scratch_shapes=[pltpu.VMEM((rows, D), bf16)],
        compiler_params=limit(28),
        cost_estimate=pl.CostEstimate(
            flops=2 * rows * (D * D + D * FF), bytes_accessed=20 * 1024 * 1024, transcendentals=0
        ),
        name="mlp_backward",
    )(lens, grad_pre, grads, after, vec, w_up, w_out)


def attention_kernel(
    qkv_ref, att_ref, mixed_ref, grad_ref, grad_proj, grad_att, means, grad_s, *, start
):
    first = lax.broadcasted_iota(jnp.int32, (1, 128), 1) < 64
    ones = jnp.ones((128, QB), bf16)
    heads = (first, jnp.logical_not(first))
    blocks = grad_proj.shape[0] // QB
    for block in range(blocks):
        span = slice(start + block * QB, start + (block + 1) * QB)
        for p in range(HEADS // 2):
            at = p * 128
            value = qkv_ref[span, 2 * D + at : 2 * D + at + 128]
            grad = grad_ref[span, at : at + 128]
            product = (grad.astype(f32) * mixed_ref[span, at : at + 128].astype(f32)).astype(bf16)
            for h, head in enumerate(heads):
                to = (block * HEADS + 2 * p + h) * QB
                grad_att[to : to + QB, :] = dot_nt(
                    jnp.where(head, grad, jnp.zeros_like(grad)), value
                )
                means[to : to + QB, :] = dot(
                    jnp.where(head, product, jnp.zeros_like(product)), ones
                )
    for block in range(blocks):
        part = slice(block * HEADS * QB, (block + 1) * HEADS * QB)
        place = (start // QB + block) * HEADS * QB
        low = att_ref[place : place + HEADS * QB, :].astype(f32)
        grad_s[part, :] = (low * (grad_att[part, :] - means[part, :])).astype(bf16)
    for block in range(blocks):
        span = slice(start + block * QB, start + (block + 1) * QB)
        dest = slice(block * QB, (block + 1) * QB)
        for p in range(HEADS // 2):
            at = p * 128
            query = qkv_ref[span, at : at + 128]
            key = qkv_ref[span, D + at : D + at + 128]
            grad = grad_ref[span, at : at + 128]
            grad_q, grad_k, grad_v = [], [], []
            for h in range(2):
                to = (block * HEADS + 2 * p + h) * QB
                place = ((start // QB + block) * HEADS + 2 * p + h) * QB
                sgrad = grad_s[to : to + QB, :]
                grad_q.append(dot(sgrad, key))
                grad_k.append(dot_tn(sgrad, query))
                grad_v.append(dot_tn(att_ref[place : place + QB, :], grad))
            for k, (parts, scale) in enumerate(((grad_q, 0.125), (grad_k, 1.0), (grad_v, 1.0))):
                grad_proj[dest, k * D + at : k * D + at + 128] = (
                    jnp.where(first, parts[0], parts[1]) * scale
                ).astype(bf16)


def input_kernel(
    proj_ref, after_ref, x_ref, vec_ref, gain_ref, bup_ref, wqkv_ref, caption_grad, sums, input_low
):
    gain_a = vec_ref[:, 0:D]
    normed_one, inverse_one = normalize(x_ref[...].astype(f32))
    input_low[...] = (normed_one * gain_a).astype(bf16)
    grad_in = dot_nt(proj_ref[...], wqkv_ref[...])
    sums[:, 0:D] = jnp.sum(grad_in * normed_one, 0, keepdims=True)
    sums[:, D : 2 * D] = jnp.sum(proj_ref[:, 0:D].astype(f32), 0, keepdims=True)
    sums[:, 2 * D : 3 * D] = jnp.sum(proj_ref[:, 2 * D :].astype(f32), 0, keepdims=True)
    sums[:, 3 * D : 4 * D] = gain_ref[...]
    sums[:, 4 * D :] = bup_ref[...]
    caption_grad[...] = after_ref[...] + norm_back(grad_in * gain_a, normed_one, inverse_one)


def proj_kernel(
    place_ref, mine_ref, proj_ref, after_ref, mixed_ref, input_ref, sums, own, other, lhs_t, grad_out
):
    chunk_rows = D // CHUNKS
    mine = mine_ref[0]
    lhs_t[...] = input_ref[...].T
    half_out, half_qkv = D // 2, 3 * D // 2
    for which, dest in ((1 - mine, other), (mine, own)):
        for col in range(0, half_qkv, 384):
            lanes = pl.ds(pl.multiple_of(which * half_qkv + col, 128), 384)
            put_chunks(dest, dot(lhs_t[...], proj_ref[:, lanes]), place_ref, col // 768, col)
    lhs_t[...] = mixed_ref[...].T
    grad_out[...] = after_ref[...].astype(bf16)
    for which, dest in ((1 - mine, other), (mine, own)):
        lanes = pl.ds(pl.multiple_of(which * half_out, 128), half_out)
        put_chunks(dest, dot(lhs_t[...], grad_out[:, lanes]), place_ref, 1, half_qkv)
    for which, dest in ((1 - mine, other), (mine, own)):
        dest[:, BW - 128 :] = jnp.zeros((D, 128), dest.dtype)
        pieces = []
        for start, size in ((0, D), (D, 2 * D), (3 * D, D), (4 * D, FF)):
            for k in range(0, size // 2, 128):
                at = pl.multiple_of(start + which * (size // 2) + k, 128)
                pieces.append(sums[:, pl.ds(at, 128)])
        pieces += [jnp.zeros_like(pieces[0])] * (32 - len(pieces))
        at = pl.multiple_of(place_ref[1, 0] * chunk_rows, 16)
        dest[pl.ds(at, 32), BW - 128 :] = jnp.concatenate(pieces, 0).astype(dest.dtype)


def rest_kernel(
    place_ref, mine_ref, qkv_ref, att_ref, mixed_ref, grad_ref, after_ref, x_ref, vec_ref,
    gain_ref, bup_ref, wqkv_ref, caption_grad, own, other,
    grad_proj, sums, input_low, grad_att, means, grad_s, lhs_t, grad_out,
):
    attention_kernel(
        qkv_ref, att_ref, mixed_ref, grad_ref, grad_proj, grad_att, means, grad_s, start=0
    )
    input_kernel(
        grad_proj, after_ref, x_ref, vec_ref, gain_ref, bup_ref, wqkv_ref,
        caption_grad, sums, input_low,
    )
    proj_kernel(
        place_ref, mine_ref, grad_proj, after_ref, mixed_ref, input_low, sums,
        own, other, lhs_t, grad_out,
    )


def rest_backward(
    place, mine, qkv, attention, mixed, grad_mixed, grad_after, captions, vec, grad_gain, grad_bup, w_qkv
):
    rows = captions.shape[0]
    shape = jax.ShapeDtypeStruct
    return pl.pallas_call(
        rest_kernel,
        out_shape=[shape((rows, D), f32), shape((D, BW), f32), shape((D, BW), bf16)],
        in_specs=[SM, SM] + [VM] * 10,
        out_specs=[VM] * 3,
        scratch_shapes=[
            pltpu.VMEM((rows, 3 * D), bf16),
            pltpu.VMEM((1, 4 * D + FF), f32),
            pltpu.VMEM((rows, D), bf16),
            pltpu.VMEM((rows * HEADS, QB), f32),
            pltpu.VMEM((rows * HEADS, QB), f32),
            pltpu.VMEM((rows * HEADS, QB), bf16),
            pltpu.VMEM((D, rows), bf16),
            pltpu.VMEM((rows, D), bf16),
        ],
        compiler_params=limit(44),
        cost_estimate=pl.CostEstimate(
            flops=2 * rows * 48 * D * D, bytes_accessed=60 * 1024 * 1024, transcendentals=0
        ),
        name="rest_backward",
    )(
        place, mine, qkv, attention, mixed, grad_mixed, grad_after, captions, vec,
        grad_gain, grad_bup, w_qkv,
    )


def dp_bits():
    bits, bit = [], 1
    while bit < lax.axis_size("dp"):
        bits.append(bit)
        bit *= 2
    return bits


def swap(values, axis, bit):
    size = lax.axis_size(axis)
    return lax.ppermute(values, axis, [(place, place ^ bit) for place in range(size)])


def gather_relative(values):
    bits = dp_bits()
    while bits:
        pair = bits[-2:]
        bits = bits[:-2]
        offsets = [0]
        for bit in pair:
            offsets += [entry + bit for entry in offsets]
        values = jnp.concatenate([swap(values, "dp", k) if k else values for k in offsets], 0)
    return jnp.concatenate([values, swap(values, "rep", 1)], 0)


def relative_chips():
    bits, table = dp_bits(), [0]
    while bits:
        pair = bits[-2:]
        bits = bits[:-2]
        offsets = [0]
        for bit in pair:
            offsets += [entry + bit for entry in offsets]
        table = [entry ^ k for k in offsets for entry in table]
    return table


def chunk_places():
    away = jnp.arange(CHUNKS, dtype=jnp.int32) ^ (lax.axis_index("dp") % CHUNKS)
    one, two, rest = away % 2, away // 2 % 2, away // 4
    return jnp.stack([one * 8 + two * 4 + rest, two * 8 + one * 4 + rest]).astype(jnp.int32)


def streams_of(width):
    return ((slice(0, width), 1, 2), (slice(width, None), 2, 1))


def reduce_first(own, arrived, streams):
    half = own.shape[0] // 2

    def both(rows, lanes):
        return own[rows, lanes] + arrived[rows, lanes].astype(f32)

    sent = [both(slice(half, None), lanes).astype(bf16) for lanes, _, _ in streams]
    return sent, [both(slice(0, half), lanes) for lanes, _, _ in streams]


def reduce_swaps(sent, streams, stage):
    return [swap(piece, "dp", stream[stage]) for piece, stream in zip(sent, streams)]


def reduce_add(came, kept):
    half = kept[0].shape[0] // 2
    totals = [total + got.astype(f32) for total, got in zip(kept, came)]
    return [total[half:].astype(bf16) for total in totals], [total[:half] for total in totals]


def reduce_join(came, kept):
    total = jnp.concatenate([total + got.astype(f32) for total, got in zip(kept, came)], 1)
    rows = total.shape[0] // 4
    return [total[k * rows : (k + 1) * rows].astype(bf16) for k in (1, 2, 3)], total[:rows]


def reduce_last(parts, total):
    total = total + sum(part.astype(f32) for part in parts)
    for bit in dp_bits()[4:]:
        total = total + swap(total.astype(bf16), "dp", bit).astype(f32)
    return total.astype(bf16)


def spread_first(chunk):
    return [swap(chunk, "dp", 4 * k) if k else chunk for k in range(4)]


def spread_second(column, streams):
    return [jnp.concatenate([piece[:, lanes] for piece in column], 0) for lanes, _, _ in streams]


def spread_swaps(pieces, streams, stage):
    return [swap(piece, "dp", stream[stage]) for piece, stream in zip(pieces, streams)]


def reduce_swaps_far(sent):
    return [swap(piece, "dp", 4 * (k + 1)) for k, piece in enumerate(sent)]


def in_quarters(*quarters):
    return [quarter[stream] for stream in range(2) for quarter in quarters]


def behind(values, others):
    return list(lax.optimization_barrier((*values, *others))[: len(values)])


def each_chunk(place_ref):
    rows = D // CHUNKS
    place = place_ref[0, 0]
    me = place // 8 + 2 * (place // 4 % 2) + 4 * (place % 4)
    for stream in range(2):
        for quarter in range(4):
            for k in range(4):
                high, low = quarter // 2, quarter % 2
                away = (high + 2 * low if stream == 0 else low + 2 * high) + 4 * k
                chunk = me ^ away
                at = pl.ds(pl.multiple_of(chunk * rows, 16), rows)
                yield stream, stream * 4 + quarter, slice(k * rows, (k + 1) * rows), chunk, at


def unpack_up_kernel(place_ref, *refs):
    parts, g_up = refs[:8], refs[8]
    for stream, part, span, _, at in each_chunk(place_ref):
        lanes = slice(stream * FF // 4, (stream + 1) * FF // 4)
        g_up[at, lanes] = parts[part][span, :].astype(f32)


def unpack_rest_kernel(place_ref, *refs):
    parts, (g_qkv, g_out), vectors = refs[:8], refs[8:10], refs[10:]
    for stream, part, span, chunk, at in each_chunk(place_ref):
        rest = parts[part][span, :].astype(f32)
        if stream == 0:
            g_qkv[at, 0:D] = rest
            continue
        g_qkv[at, D:] = rest[:, : D // 2]
        g_out[at, :] = rest[:, D // 2 : D]

        @pl.when(chunk == 0)
        def _():
            row = 0
            for dest in vectors:
                for lane in range(0, dest.shape[0], 128):
                    dest[lane : lane + 128] = rest[row, D:]
                    row += 1


def unpack_up(place, parts):
    return pl.pallas_call(
        unpack_up_kernel,
        out_shape=jax.ShapeDtypeStruct((D, FF // 2), f32),
        in_specs=[SM] + [VM] * 8,
        out_specs=VM,
        compiler_params=limit(20),
        name="unpack_up",
    )(place, *parts)


def unpack_rest(place, parts):
    shape = jax.ShapeDtypeStruct
    return pl.pallas_call(
        unpack_rest_kernel,
        out_shape=[
            shape((D, 3 * D // 2), f32),
            shape((D, D // 2), f32),
            shape((D // 2,), f32),
            shape((D,), f32),
            shape((D // 2,), f32),
            shape((FF // 2,), f32),
        ],
        in_specs=[SM] + [VM] * 8,
        out_specs=[VM] * 6,
        compiler_params=limit(20),
        name="unpack_rest",
    )(place, *parts)


def softmax_parts(scores, axis):
    maxima = jnp.max(scores, axis, keepdims=True)
    powers = jnp.exp(scores - maxima)
    totals = jnp.sum(powers, axis, keepdims=True)
    return powers / totals, maxima + jnp.log(totals)


def text_unit(pooled_low, text_proj):
    proj_out = dot(pooled_low, text_proj)
    inverse_z = lax.rsqrt(jnp.sum(proj_out * proj_out, -1, keepdims=True) + EPS)
    return proj_out * inverse_z, inverse_z


def branch_grad(grad_unit, unit_text, inverse_z, text_proj, lengths):
    grad_projout = (
        inverse_z * (grad_unit - unit_text * jnp.sum(unit_text * grad_unit, -1, keepdims=True))
    ).astype(bf16)
    return dot_nt(grad_projout, text_proj) / lengths


def loss_kernel(
    where_ref, early_ref, image_ref, proj_ref, pair_loss, own_grads, own_branch, branch,
    unit, inverse, scores, sgrad,
):
    total = image_ref.shape[0]
    number = own_grads.shape[0]
    chip, mine = where_ref[0], where_ref[1]
    block = 256
    for row in range(0, total, block):
        span = slice(row, row + block)
        proj_out = dot(early_ref[span, 0:D], proj_ref[...])
        inverse_z = lax.rsqrt(jnp.sum(proj_out * proj_out, -1, keepdims=True) + EPS)
        inverse[span, :] = jnp.broadcast_to(inverse_z, (block, 128))
        unit[span, :] = proj_out * inverse_z
        scores[span, :] = dot_nt(unit[span, :].astype(bf16), image_ref[...]) * SCALE
    place = lax.broadcasted_iota(jnp.int32, (1, total), 1) // number
    chips = total // (2 * number)
    away = place % chips
    other = place // chips
    from_chip = chip ^ (away // 4 + 4 * (away % 4)) if chips == 16 else None
    image_id = (from_chip * 2 + (mine ^ other)) * number + (
        lax.broadcasted_iota(jnp.int32, (1, total), 1) % number
    )
    column_max = jnp.max(scores[...], 0, keepdims=True)
    column_sum = jnp.zeros((1, total), f32)
    for row in range(0, total, block):
        column_sum += jnp.sum(
            jnp.exp(scores[row : row + block, :] - column_max), 0, keepdims=True
        )
    column_total = column_max + jnp.log(column_sum)
    for row in range(0, total, block):
        span = slice(row, row + block)
        values = scores[span, :]
        row_max = jnp.max(values, 1, keepdims=True)
        powers = jnp.exp(values - row_max)
        by_text = powers * (0.5 / jnp.sum(powers, 1, keepdims=True))
        by_image = jnp.exp(values - column_max) * (0.5 / column_sum)
        text_id = lax.broadcasted_iota(jnp.int32, (block, 1), 0) + row
        same = jnp.where(text_id == image_id, 1.0, 0.0)
        sgrad[span, :] = (by_text + by_image - same).astype(bf16)
        grad_unit = dot(sgrad[span, :], image_ref[...]) * SCALE
        unit_text = unit[span, :]
        grad_proj = (
            inverse[span, 0:1]
            * (grad_unit - unit_text * jnp.sum(unit_text * grad_unit, -1, keepdims=True))
        ).astype(bf16)
        unit[span, :] = dot_nt(grad_proj, proj_ref[...]) / early_ref[span, D : D + 1].astype(f32)
        branch[span, :] = unit[span, :].astype(bf16)
    first = pl.multiple_of((chip * 2 + mine) * number, 32)
    own_grads[...] = unit[pl.ds(first, number), :]
    own_branch[...] = unit[pl.ds(first, number), :].astype(bf16)
    values = scores[pl.ds(first, number), :]
    row_max = jnp.max(values, 1, keepdims=True)
    row_total = row_max + jnp.log(jnp.sum(jnp.exp(values - row_max), 1, keepdims=True))
    text_id = lax.broadcasted_iota(jnp.int32, (number, 1), 0) + first
    same = jnp.where(text_id == image_id, 1.0, 0.0)
    both = 0.5 * (row_total + column_total) - values
    pair_loss[...] = jnp.broadcast_to(jnp.sum(both * same, 1, keepdims=True), (number, 128))


def loss_whole(early_all, image_all, text_proj, chip, mine, number):
    total = image_all.shape[0]
    shape = jax.ShapeDtypeStruct
    pair_loss, grads, own_branch, branch = pl.pallas_call(
        loss_kernel,
        out_shape=[
            shape((number, 128), f32),
            shape((number, D), f32),
            shape((number, D), bf16),
            shape((total, D), bf16),
        ],
        in_specs=[SM] + [VM] * 3,
        out_specs=[VM] * 4,
        scratch_shapes=[
            pltpu.VMEM((total, D), f32),
            pltpu.VMEM((total, 128), f32),
            pltpu.VMEM((total, total), f32),
            pltpu.VMEM((total, total), bf16),
        ],
        compiler_params=limit(26),
        name="pair_loss",
    )(jnp.stack([chip, mine]), early_all[:, :EARLY], image_all, text_proj)
    return pair_loss[:, 0], grads, own_branch, branch


def loss_rows(pooled_all, image_all, text_proj, lengths_all, image_ids, first_row, local_pairs):
    unit_all, inverse_all = text_unit(pooled_all, text_proj)

    def own_rows(values):
        return lax.dynamic_slice_in_dim(values, first_row, local_pairs, 0)

    unit_text, inverse_z = own_rows(unit_all), own_rows(inverse_all)
    text_scores = dot_nt(unit_text.astype(bf16), image_all) * SCALE
    image_scores = dot_nt(image_all[:local_pairs], unit_all.astype(bf16)) * SCALE
    by_text, text_total = softmax_parts(text_scores, 1)
    image_total = softmax_parts(image_scores, 1)[1]
    every_total = gather_relative(image_total)
    text_ids = first_row + jnp.arange(local_pairs, dtype=jnp.int32)
    own_same = (text_ids[:, None] == image_ids).astype(f32)
    own = jnp.sum(text_scores * own_same, -1)
    pair_loss = 0.5 * (text_total[:, 0] - own) + 0.5 * (image_total[:, 0] - own)
    by_image = jnp.exp(text_scores - every_total[:, 0][None, :])
    sgrad = (0.5 * (by_text - own_same) + 0.5 * (by_image - own_same)).astype(bf16)
    grad_unit = dot(sgrad, image_all) * SCALE
    grads = branch_grad(grad_unit, unit_text, inverse_z, text_proj, own_rows(lengths_all))
    return pair_loss, grads, grads.astype(bf16), grads.astype(bf16)


def local(
    images,
    groups,
    captions,
    cap_lengths,
    img_gain_a,
    img_w_qkv,
    img_b_qv,
    img_w_out,
    img_gain_m,
    img_w_up,
    img_b_up,
    img_w_down,
    gain_attn,
    w_qkv,
    b_qv,
    w_out,
    gain_mlp,
    w_up,
    b_up,
    w_down,
    text_proj,
):
    local_pairs = images.shape[0]
    rows_total = local_pairs * CAP
    mine = lax.axis_index("rep").astype(jnp.int32)
    mine_one = mine[None]
    total_pairs = local_pairs * lax.axis_size("dp") * lax.axis_size("rep")
    whole = total_pairs <= MOST_PAIRS

    image_vec = jnp.concatenate([img_gain_a, img_b_qv, img_gain_m, img_b_up])[None]
    image_vec_other = swap(image_vec, "rep", 1)
    weights = []
    for weight in (img_w_qkv, img_w_out, img_w_up, img_w_down):
        weights += [weight, swap(weight, "rep", 1)]

    text_vec = lax.optimization_barrier(jnp.concatenate([gain_attn, b_qv, gain_mlp, b_up]))
    text_vec = text_vec.astype(f32)[None]
    flat = captions.reshape(rows_total, D)
    qkv, mixed, after, mlp, slope, attention, early = text_forward(
        flat, cap_lengths, text_vec, w_qkv, w_out, w_up, w_down
    )
    early, image_vec_other, *weights = lax.optimization_barrier((early, image_vec_other, *weights))
    early_all = lax.all_gather(
        early if whole else early[:, :EARLY], ("dp", "rep"), axis=0, tiled=True
    )
    image_emb = image_tower(
        jnp.transpose(images, (1, 0, 2)), groups, mine_one, image_vec, image_vec_other, weights
    )
    image_all = gather_relative(image_emb)
    chip = lax.axis_index("dp").astype(jnp.int32)
    if whole:
        pair_loss, grads, branch, branch_all = loss_whole(
            early_all, image_all, text_proj, chip, mine, local_pairs
        )
    else:
        chips = chip ^ jnp.array(relative_chips(), jnp.int32)
        devices = jnp.concatenate([2 * chips + mine, 2 * chips + 1 - mine])
        image_ids = (
            devices[:, None] * local_pairs + jnp.arange(local_pairs, dtype=jnp.int32)[None, :]
        ).reshape(1, total_pairs)
        pair_loss, grads, branch, branch_all = loss_rows(
            early_all[:, :D],
            image_all,
            text_proj,
            early_all[:, D : D + 1].astype(f32),
            image_ids,
            (2 * chip + mine) * local_pairs,
            local_pairs,
        )
    place = chunk_places()
    grad_pre, up_own, up_other, grad_bup = up_backward(
        place, mine_one, cap_lengths, branch, slope, mlp, w_down
    )
    arrived = swap(up_other, "rep", 1)
    grad_after, grad_mixed, grad_gain = mlp_backward(
        cap_lengths, grad_pre, grads, after, text_vec, w_up, w_out
    )
    ups, rests = streams_of(FF // 4), streams_of(D)
    up_sent, up_kept = reduce_first(up_own, arrived, ups)
    (grad_mixed,) = behind([grad_mixed], up_sent)
    up_came = reduce_swaps(up_sent, ups, 1)
    caption_grad, rest_own, rest_other = rest_backward(
        place, mine_one, qkv, attention, mixed, grad_mixed, grad_after, flat, text_vec,
        grad_gain, grad_bup, w_qkv,
    )
    rest_other, *up_came = lax.optimization_barrier((rest_other, *up_came))
    arrived = swap(rest_other, "rep", 1)
    up_sent, up_kept = reduce_add(up_came, up_kept)
    up_came = reduce_swaps(up_sent, ups, 2)
    (arrived,) = behind([arrived], up_sent)
    rest_sent, rest_kept = reduce_first(rest_own, arrived, rests)
    rest_came = reduce_swaps(rest_sent, rests, 1)
    up_came = behind(up_came, rest_sent)
    up_sent, up_kept = reduce_join(up_came, up_kept)
    up_came = reduce_swaps_far(up_sent)
    (branch_all,) = behind([branch_all], up_sent)
    half = D // 2
    own_columns = lax.dynamic_slice_in_dim(branch_all, mine * half, half, 1)
    if whole:
        grad_w_down = dot_tn(early_all[:, EARLY:], own_columns)
    else:
        other_columns = lax.dynamic_slice_in_dim(branch_all, (1 - mine) * half, half, 1)
        grad_w_down = dot_tn(early[:, EARLY:], own_columns) + swap(
            dot_tn(early[:, EARLY:], other_columns).astype(bf16), "rep", 1
        ).astype(f32)
        grad_w_down = lax.psum(grad_w_down, "dp")
    rest_came = behind(rest_came, [grad_w_down])
    rest_sent, rest_kept = reduce_add(rest_came, rest_kept)
    rest_came = reduce_swaps(rest_sent, rests, 2)
    up_came = behind(up_came, rest_sent)
    up_chunk = reduce_last(up_came, up_kept)
    up_column = spread_first(up_chunk)
    rest_came = behind(rest_came, [up_chunk])
    rest_sent, rest_kept = reduce_join(rest_came, rest_kept)
    rest_came = reduce_swaps_far(rest_sent)
    up_column = behind(up_column, rest_sent)
    up_mine = spread_second(up_column, ups)
    up_near, up_across = spread_swaps(up_mine, ups, 2), spread_swaps(up_mine, ups, 1)
    rest_came = behind(rest_came, up_near + up_across)
    rest_chunk = reduce_last(rest_came, rest_kept)
    rest_column = spread_first(rest_chunk)
    up_near = behind(up_near, [rest_chunk])
    up_last = spread_swaps(up_near, ups, 1)
    rest_column = behind(rest_column, up_near)
    rest_mine = spread_second(rest_column, rests)
    rest_near, rest_across = spread_swaps(rest_mine, rests, 2), spread_swaps(rest_mine, rests, 1)
    up_last = behind(up_last, rest_mine)
    grad_w_up = unpack_up(place, in_quarters(up_mine, up_near, up_across, up_last))
    rest_near = behind(rest_near, [grad_w_up])
    rest_last = spread_swaps(rest_near, rests, 1)
    grad_w_qkv, grad_w_out, *small = unpack_rest(
        place, in_quarters(rest_mine, rest_near, rest_across, rest_last)
    )
    return (
        pair_loss,
        caption_grad.reshape(local_pairs, CAP, D),
        small[0],
        grad_w_qkv,
        small[1],
        grad_w_out,
        small[2],
        grad_w_up,
        small[3],
        grad_w_down,
    )


def solution(mesh):
    in_specs = (
        P(("dp", "rep"), None, None),
        P(("dp", "rep")),
        P(("dp", "rep"), None, None),
        P(("dp", "rep")),
        P("rep"),
        P("rep", None),
        P("rep"),
        P("rep", None),
        P("rep"),
        P("rep", None),
        P("rep"),
        P("rep", None),
        P(),
        P(),
        P(),
        P(),
        P(),
        P(),
        P(),
        P(),
        P(),
    )
    out_specs = (
        P(("dp", "rep")),
        P(("dp", "rep"), None, None),
        P("rep"),
        P(None, "rep"),
        P("rep"),
        P(None, "rep"),
        P("rep"),
        P(None, "rep"),
        P("rep"),
        P(None, "rep"),
    )
    return jax.shard_map(local, mesh=mesh, in_specs=in_specs, out_specs=out_specs, check_vma=False)
```

profile of v0, /device:TPU:8, one launch (start us, length us, event | category | flops | bytes accessed | tf_op | source)
XLA Modules:
  0.0 296.8 jit_solution(4580735727619190961)
XLA Ops:
  10.6 17.2 %text_forward.1 = (bf16[512,2304]{1,0:T(8,128)(2,1)}, bf16[512,768]{1,0:T(8,128)(2,1)}, f32[512,768]{1,0:T(8,128)}, bf16[512,768]{1,0:T(8,128)(2,1)}, bf16[512,3...) custom-call(s32[32]{0:T(128)} %lens_ref.5, bf16[512,768]{1,0:T(8,128)(2,1)} %bitcast.11, ...), custom_call_target="tpu_custom_call" | custom-call | flops 7247757312 | bytes 25165824 | tf_op jit(solution)/shard_map/text_forward/pallas_call | solution.py:508
  29.8 86.3 %image_tower.1 = bf16[32,768]{1,0:T(8,128)(2,1)} custom-call(s32[32]{0:T(128)} %groups_ref.1, s32[1]{0:T(128)} %bitcast.1.mine_ref, bf16[145,32,768]{2,1,0:T(8,128)(2,1)} %bitcast.13, bf16[1,3072]{1,0:T(2,128)(2,1)} %copy-done.17, bf16[1,3072]{1,0:T(2,128)(2,1)} %copy-done.20, bf16[384,2304]{1,0:T(8,128)(2,1)} %qkv_own, bf16[384,2304]{1,0:T(8,128)(2,1)} %copy-done.18, ...), custom_call_target="tpu_custom_call" | custom-call | flops 30198988800 | bytes 25165824 | tf_op jit(solution)/shard_map/image_tower/pallas_call | solution.py:360
  116.3 3.4 %collective-permute-start.7 = (bf16[32,768]{1,0:T(8,128)(2,1)}, bf16[32,768]{1,0:T(8,128)(2,1)S(1)}, u32[]{:S(2)}, u32[]{:S(2)}) collective-permute-start(bf16[32,768]{1,0:T(8,128)(2,1)} %image_tower.1), channel_id=1, source_target_pairs={{0,24},{2,26},{4,28},{6,30},{8,16},{10,18},{12,20},{14,22},{16,8},... | collective-permute-start | bytes 147464 | tf_op jit(solution)/shard_map/ppermute | solution.py:778
  124.0 3.4 %collective-permute-start.10 = (bf16[128,768]{1,0:T(8,128)(2,1)S(1)}, bf16[128,768]{1,0:T(8,128)(2,1)S(1)}, u32[]{:S(2)}, u32[]{:S(2)}) collective-permute-start(bf16[128,768]{1,0:T(8,128)(2,1)S(1)} %pad_maximum_fusion.6), channel_id=1, source_target_pairs={{0,6},{2,4},{4,2},{6,0},{8,14},{10,12},{12,10},{14,8},{16,22},{18,... | collective-permute-start | bytes 589832 | tf_op jit(solution)/shard_map/ppermute | solution.py:778
  129.6 2.2 collective-permute-done.9
  131.9 4.0 %collective-permute-start.11 = (bf16[512,768]{1,0:T(8,128)(2,1)S(1)}, bf16[512,768]{1,0:T(8,128)(2,1)S(1)}, u32[]{:S(2)}, u32[]{:S(2)}) collective-permute-start(bf16[512,768]{1,0:T(8,128)(2,1)S(1)} %get-tuple-element.158), channel_id=1, source_target_pairs={{0,1},{1,0},{2,3},{3,2},{4,5},{5,4},{6,7},{7,6},{8,9},{9,8},{10,11... | collective-permute-start | bytes 2359304 | tf_op jit(solution)/shard_map/ppermute | solution.py:778
  139.8 11.7 %pair_loss.1 = (f32[32,128]{1,0:T(8,128)S(1)}, f32[32,768]{1,0:T(8,128)S(1)}, bf16[32,768]{1,0:T(8,128)(2,1)S(1)}, bf16[1024,768]{1,0:T(8,128)(2,1)S(1)}) custom-call(s32[2]{0:T(128)S(1)} %pad_add_fusion.1.where_ref, bf16[1024,896]{1,0:T(8,128)(2,1)S(1)} %slice.214.early_ref, bf16[1024,768]{1,0:T(8,128)(2,1)S(1)} %constant_dynamic-update-slice_fusion.7.image_ref, ...), custom_call_target="tpu_custom_call" | custom-call | tf_op jit(solution)/shard_map/pair_loss/pallas_call | solution.py:1025
  155.7 6.5 %up_backward.1 = (bf16[512,3072]{1,0:T(8,128)(2,1)S(1)}, f32[768,1536]{1,0:T(8,128)S(1)}, bf16[768,1536]{1,0:T(8,128)(2,1)S(1)}, f32[1,3072]{1,0:T(1,128)S(1)}) custom-call(s32[2,16]{1,0:T(2,128)S(1)} %pad_add_fusion.place_ref, s32[1]{0:T(128)} %bitcast.1.mine_ref, s32[32]{0:T(128)S(1)} %copy-done.8, bf16[32,768]{1,0:T(8,128)(2,1)S(1)} %get-tuple-element.94.branch_ref, ...), custom_call_target="tpu_custom_call" | custom-call | flops 2415919104 | bytes 20971520 | tf_op jit(solution)/shard_map/up_backward/pallas_call | solution.py:571
  162.7 5.6 %mlp_backward.1 = (f32[512,768]{1,0:T(8,128)S(1)}, bf16[512,768]{1,0:T(8,128)(2,1)S(1)}, f32[1,768]{1,0:T(1,128)S(1)}) custom-call(s32[32]{0:T(128)S(1)} %copy-done.8, bf16[512,3072]{1,0:T(8,128)(2,1)S(1)} %get-tuple-element.97.pre_ref, f32[32,768]{1,0:T(8,128)S(1)} %get-tuple-element.98.grad_ref, f32[512,768]{1,0:T(8,128)S(1)} %copy-done.11, ...), custom_call_target="tpu_custom_call" | custom-call | flops 3019898880 | bytes 20971520 | tf_op jit(solution)/shard_map/mlp_backward/pallas_call | solution.py:613
  172.5 14.5 %rest_backward.1 = (f32[512,768]{1,0:T(8,128)}, f32[768,1664]{1,0:T(8,128)}, bf16[768,1664]{1,0:T(8,128)(2,1)}) custom-call(s32[2,16]{1,0:T(2,128)S(1)} %pad_add_fusion.place_ref, s32[1]{0:T(128)} %bitcast.1.mine_ref, bf16[512,2304]{1,0:T(8,128)(2,1)S(1)} %copy-done.12, bf16[6144,128]{1,0:T(8,128)(2,1)S(1)} %copy-done.13, bf16[512,768]{1,0:T(8,128)(2,1)S(1)} %copy-done.14, ...), custom_call_target="tpu_custom_call" | custom-call | flops 28991029248 | bytes 62914560 | tf_op jit(solution)/shard_map/rest_backward/pallas_call | solution.py:742
  187.0 2.6 convert_add_fusion.2
  194.3 5.3 %collective-permute-done.18 = bf16[192,768]{1,0:T(8,128)(2,1)S(1)} collective-permute-done((bf16[192,768]{1,0:T(8,128)(2,1)S(1)}, bf16[192,768]{1,0:T(8,128)(2,1)S(1)}, u32[]{:S(2)}, u32[]{:S(2)}) %collective-permute-start.18) | collective-permute-done | bytes 294944 | tf_op jit(solution)/shard_map/ppermute | solution.py:778
  204.7 8.4 %fusion = f32[3072,384]{1,0:T(8,128)} fusion(bf16[1024,3968]{1,0:T(8,128)(2,1)} %all-gather.2.cloned.1.call-done, bf16[1024,768]{1,0:T(8,128)(2,1)S(1)} %copy-done.5, s32[]{:T(128)S(6)} %select_n.77), kind=kOutput, calls=%fused_computation | convolution fusion | flops 2415919104 | bytes 11796484 | tf_op jit(solution)/shard_map/dot_general | solution.py:48
  220.1 3.1 %collective-permute-done.20 = bf16[192,768]{1,0:T(8,128)(2,1)S(1)} collective-permute-done((bf16[192,768]{1,0:T(8,128)(2,1)S(1)}, bf16[192,768]{1,0:T(8,128)(2,1)S(1)}, u32[]{:S(2)}, u32[]{:S(2)}) %collective-permute-start.20) | collective-permute-done | bytes 294944 | tf_op jit(solution)/shard_map/ppermute | solution.py:778
  230.0 7.5 %collective-permute-done.30 = bf16[48,1536]{1,0:T(8,128)(2,1)S(1)} collective-permute-done((bf16[48,1536]{1,0:T(8,128)(2,1)S(1)}, bf16[48,1536]{1,0:T(8,128)(2,1)S(1)}, u32[]{:S(2)}, u32[]{:S(2)}) %collective-permute-start.30) | collective-permute-done | bytes 147488 | tf_op jit(solution)/shard_map/ppermute | solution.py:778
  243.2 5.2 %collective-permute-done.27 = bf16[48,1664]{1,0:T(8,128)(2,1)S(1)} collective-permute-done((bf16[48,1664]{1,0:T(8,128)(2,1)S(1)}, bf16[48,1664]{1,0:T(8,128)(2,1)S(1)}, u32[]{:S(2)}, u32[]{:S(2)}) %collective-permute-start.27) | collective-permute-done | bytes 159776 | tf_op jit(solution)/shard_map/ppermute | solution.py:778
  248.6 7.0 %collective-permute-start.36 = (bf16[48,1664]{1,0:T(8,128)(2,1)S(1)}, bf16[48,1664]{1,0:T(8,128)(2,1)S(1)}, u32[]{:S(2)}, u32[]{:S(2)}) collective-permute-start(bf16[48,1664]{1,0:T(8,128)(2,1)S(1)} %fusion.7), channel_id=1, source_target_pairs={{0,16},{2,18},{4,20},{6,22},{8,24},{10,26},{12,28},{14,30},{16,0},... | collective-permute-start | bytes 479240 | tf_op jit(solution)/shard_map/ppermute | solution.py:778
  258.2 3.1 %collective-permute-done.36 = bf16[48,1664]{1,0:T(8,128)(2,1)S(1)} collective-permute-done((bf16[48,1664]{1,0:T(8,128)(2,1)S(1)}, bf16[48,1664]{1,0:T(8,128)(2,1)S(1)}, u32[]{:S(2)}, u32[]{:S(2)}) %collective-permute-start.36) | collective-permute-done | bytes 159776 | tf_op jit(solution)/shard_map/ppermute | solution.py:778
  261.3 2.7 collective-permute-done.37
  268.1 3.1 %unpack_up.1 = f32[768,1536]{1,0:T(8,128)} custom-call(s32[2,16]{1,0:T(2,128)S(1)} %pad_add_fusion.place_ref, bf16[192,768]{1,0:T(8,128)(2,1)S(1)} %pad_maximum_fusion.3.refs_0_, bf16[192,768]{1,0:T(8,128)(2,1)S(1)} %collective-permute-done.31.refs_1_, bf16[192,768]{1,0:T(8,128)(2,1)S(1)} %collective-permute-done.33.refs_2_, ...), custom_call_target="tpu_custom_call" | custom-call | tf_op jit(solution)/shard_map/unpack_up/pallas_call | solution.py:913
  271.2 4.2 %collective-permute-done.38.refs_1_ = bf16[192,768]{1,0:T(8,128)(2,1)S(1)} collective-permute-done((bf16[192,768]{1,0:T(8,128)(2,1)S(1)}, bf16[192,768]{1,0:T(8,128)(2,1)S(1)}, u32[]{:S(2)}, u32[]{:S(2)}) %collective-permute-start.38) | collective-permute-done | bytes 294944 | tf_op jit(solution)/shard_map/ppermute | solution.py:778
  279.4 4.1 %collective-permute-done.42.refs_2_ = bf16[192,768]{1,0:T(8,128)(2,1)S(1)} collective-permute-done((bf16[192,768]{1,0:T(8,128)(2,1)S(1)}, bf16[192,768]{1,0:T(8,128)(2,1)S(1)}, u32[]{:S(2)}, u32[]{:S(2)}) %collective-permute-start.42) | collective-permute-done | bytes 294944 | tf_op jit(solution)/shard_map/ppermute | solution.py:778
  283.4 3.2 %collective-permute-done.43.refs_3_ = bf16[192,768]{1,0:T(8,128)(2,1)S(1)} collective-permute-done((bf16[192,768]{1,0:T(8,128)(2,1)S(1)}, bf16[192,768]{1,0:T(8,128)(2,1)S(1)}, u32[]{:S(2)}, u32[]{:S(2)}) %collective-permute-start.43) | collective-permute-done | bytes 294944 | tf_op jit(solution)/shard_map/ppermute | solution.py:778
  286.6 3.1 %unpack_rest.1 = (f32[768,1152]{1,0:T(8,128)}, f32[768,384]{1,0:T(8,128)}, f32[384]{0:T(512)}, f32[768]{0:T(1024)}, f32[384]{0:T(512)}, /*index=5*/f32[1536]{0:T(1024)}) custom-call(s32[2,16]{1,0:T(2,128)S(1)} %pad_add_fusion.place_ref, bf16[192,768]{1,0:T(8,128)(2,1)S(1)} %pad_maximum_fusion.5.refs_0_, ...), custom_call_target="tpu_custom_call" | custom-call | tf_op jit(solution)/shard_map/unpack_rest/pallas_call | solution.py:925
  (181 shorter events, 64.5 us)
Async XLA Ops:
  7.2 130.8 %all-gather.2.cloned.1.call-start = ((), (), s32[]{:S(2)}) async-start(), calls=%async_computation | async-start | bytes 8380416 | tf_op jit(solution)/shard_map/all_gather | solution.py:1113
  7.2 21.4 %collective-permute-start.3 = (bf16[384,3072]{1,0:T(8,128)(2,1)}, bf16[384,3072]{1,0:T(8,128)(2,1)}, u32[]{:S(2)}, u32[]{:S(2)}) collective-permute-start(bf16[384,3072]{1,0:T(8,128)(2,1)} %up_own), channel_id=1, source_target_pairs={{0,1},{1,0},{2,3},{3,2},{4,5},{5,4},{6,7},{7,6},{8,9},{9,8},{10,11... | collective-permute-start | bytes 7077896 | tf_op jit(solution)/shard_map/ppermute | solution.py:778
  7.3 21.3 %collective-permute-start.4 = (bf16[1536,768]{1,0:T(8,128)(2,1)}, bf16[1536,768]{1,0:T(8,128)(2,1)}, u32[]{:S(2)}, u32[]{:S(2)}) collective-permute-start(bf16[1536,768]{1,0:T(8,128)(2,1)} %down_own), channel_id=1, source_target_pairs={{0,1},{1,0},{2,3},{3,2},{4,5},{5,4},{6,7},{7,6},{8,9},{9,8},{10,11... | collective-permute-start | bytes 7077896 | tf_op jit(solution)/shard_map/ppermute | solution.py:778
  7.8 20.0 %collective-permute-start.1 = (bf16[384,2304]{1,0:T(8,128)(2,1)}, bf16[384,2304]{1,0:T(8,128)(2,1)S(1)}, u32[]{:S(2)}, u32[]{:S(2)}) collective-permute-start(bf16[384,2304]{1,0:T(8,128)(2,1)} %qkv_own), channel_id=1, source_target_pairs={{0,1},{1,0},{2,3},{3,2},{4,5},{5,4},{6,7},{7,6},{8,9},{9,8},{10,11... | collective-permute-start | bytes 5308424 | tf_op jit(solution)/shard_map/ppermute | solution.py:778
  8.6 19.1 %collective-permute-start = (bf16[1,3072]{1,0:T(2,128)(2,1)S(1)}, bf16[1,3072]{1,0:T(2,128)(2,1)S(1)}, u32[]{:S(2)}, u32[]{:S(2)}) collective-permute-start(bf16[1,3072]{1,0:T(2,128)(2,1)S(1)} %broadcast_in_dim.11.vec_own_ref), channel_id=1, source_target_pairs={{0,1},{1,0},{2,3},{3,2},{4,5},{5,4},{6,7},{7,6},{8,9},{9,8},{10,11... | collective-permute-start | bytes 18440 | tf_op jit(solution)/shard_map/ppermute | solution.py:778
  9.1 18.6 %collective-permute-start.2 = (bf16[384,768]{1,0:T(8,128)(2,1)}, bf16[384,768]{1,0:T(8,128)(2,1)S(1)}, u32[]{:S(2)}, u32[]{:S(2)}) collective-permute-start(bf16[384,768]{1,0:T(8,128)(2,1)} %out_own), channel_id=1, source_target_pairs={{0,1},{1,0},{2,3},{3,2},{4,5},{5,4},{6,7},{7,6},{8,9},{9,8},{10,11... | collective-permute-start | bytes 1769480 | tf_op jit(solution)/shard_map/ppermute | solution.py:778
  169.7 17.2 %collective-permute-start.13 = (bf16[384,768]{1,0:T(8,128)(2,1)S(1)}, bf16[384,768]{1,0:T(8,128)(2,1)S(1)}, u32[]{:S(2)}, u32[]{:S(2)}) collective-permute-start(bf16[384,768]{1,0:T(8,128)(2,1)S(1)} %get-tuple-element.151), channel_id=1, source_target_pairs={{0,2},{2,0},{4,6},{6,4},{8,10},{10,8},{12,14},{14,12},{16,18},{18,... | collective-permute-start | bytes 1769480 | tf_op jit(solution)/shard_map/ppermute | solution.py:778
  171.7 15.3 %collective-permute-start.14 = (bf16[384,768]{1,0:T(8,128)(2,1)S(1)}, bf16[384,768]{1,0:T(8,128)(2,1)}, u32[]{:S(2)}, u32[]{:S(2)}) collective-permute-start(bf16[384,768]{1,0:T(8,128)(2,1)S(1)} %get-tuple-element.150), channel_id=1, source_target_pairs={{0,4},{2,6},{4,0},{6,2},{8,12},{10,14},{12,8},{14,10},{16,20},{18,... | collective-permute-start | bytes 1769480 | tf_op jit(solution)/shard_map/ppermute | solution.py:778
  192.2 21.0 %collective-permute-start.16 = (bf16[384,768]{1,0:T(8,128)(2,1)S(1)}, bf16[384,768]{1,0:T(8,128)(2,1)S(1)}, u32[]{:S(2)}, u32[]{:S(2)}) collective-permute-start(bf16[384,768]{1,0:T(8,128)(2,1)S(1)} %add_convert_fusion.1), channel_id=1, source_target_pairs={{0,2},{2,0},{4,6},{6,4},{8,10},{10,8},{12,14},{14,12},{16,18},{18,... | collective-permute-start | bytes 1769480 | tf_op jit(solution)/shard_map/ppermute | solution.py:778
  193.5 20.5 %collective-permute-start.17 = (bf16[384,896]{1,0:T(8,128)(2,1)S(1)}, bf16[384,896]{1,0:T(8,128)(2,1)S(1)}, u32[]{:S(2)}, u32[]{:S(2)}) collective-permute-start(bf16[384,896]{1,0:T(8,128)(2,1)S(1)} %add_convert_fusion), channel_id=1, source_target_pairs={{0,4},{2,6},{4,0},{6,2},{8,12},{10,14},{12,8},{14,10},{16,20},{18,... | collective-permute-start | bytes 2064392 | tf_op jit(solution)/shard_map/ppermute | solution.py:778
  201.2 15.3 %collective-permute-start.22 = (bf16[48,1536]{1,0:T(8,128)(2,1)S(1)}, bf16[48,1536]{1,0:T(8,128)(2,1)S(1)}, u32[]{:S(2)}, u32[]{:S(2)}) collective-permute-start(bf16[48,1536]{1,0:T(8,128)(2,1)S(1)} %get-tuple-element.157), channel_id=1, source_target_pairs={{0,8},{2,10},{4,12},{6,14},{8,0},{10,2},{12,4},{14,6},{16,24},{18,... | collective-permute-start | bytes 442376 | tf_op jit(solution)/shard_map/ppermute | solution.py:778
  202.6 13.8 %collective-permute-start.23 = (bf16[48,1536]{1,0:T(8,128)(2,1)S(1)}, bf16[48,1536]{1,0:T(8,128)(2,1)S(1)}, u32[]{:S(2)}, u32[]{:S(2)}) collective-permute-start(bf16[48,1536]{1,0:T(8,128)(2,1)S(1)} %get-tuple-element.156), channel_id=1, source_target_pairs={{0,16},{2,18},{4,20},{6,22},{8,24},{10,26},{12,28},{14,30},{16,0},... | collective-permute-start | bytes 442376 | tf_op jit(solution)/shard_map/ppermute | solution.py:778
  204.2 12.3 %collective-permute-start.24 = (bf16[48,1536]{1,0:T(8,128)(2,1)S(1)}, bf16[48,1536]{1,0:T(8,128)(2,1)S(1)}, u32[]{:S(2)}, u32[]{:S(2)}) collective-permute-start(bf16[48,1536]{1,0:T(8,128)(2,1)S(1)} %get-tuple-element.155), channel_id=1, source_target_pairs={{0,24},{2,26},{4,28},{6,30},{8,16},{10,18},{12,20},{14,22},{16,8},... | collective-permute-start | bytes 442376 | tf_op jit(solution)/shard_map/ppermute | solution.py:778
  216.5 12.0 %collective-permute-start.28 = (bf16[48,1536]{1,0:T(8,128)(2,1)S(1)}, bf16[48,1536]{1,0:T(8,128)(2,1)S(1)}, u32[]{:S(2)}, u32[]{:S(2)}) collective-permute-start(bf16[48,1536]{1,0:T(8,128)(2,1)S(1)} %fusion.10), channel_id=1, source_target_pairs={{0,8},{2,10},{4,12},{6,14},{8,0},{10,2},{12,4},{14,6},{16,24},{18,... | collective-permute-start | bytes 442376 | tf_op jit(solution)/shard_map/ppermute | solution.py:778
  218.2 11.8 %collective-permute-start.29 = (bf16[48,1536]{1,0:T(8,128)(2,1)S(1)}, bf16[48,1536]{1,0:T(8,128)(2,1)S(1)}, u32[]{:S(2)}, u32[]{:S(2)}) collective-permute-start(bf16[48,1536]{1,0:T(8,128)(2,1)S(1)} %fusion.10), channel_id=1, source_target_pairs={{0,16},{2,18},{4,20},{6,22},{8,24},{10,26},{12,28},{14,30},{16,0},... | collective-permute-start | bytes 442376 | tf_op jit(solution)/shard_map/ppermute | solution.py:778
  219.6 17.9 %collective-permute-start.30 = (bf16[48,1536]{1,0:T(8,128)(2,1)S(1)}, bf16[48,1536]{1,0:T(8,128)(2,1)S(1)}, u32[]{:S(2)}, u32[]{:S(2)}) collective-permute-start(bf16[48,1536]{1,0:T(8,128)(2,1)S(1)} %fusion.10), channel_id=1, source_target_pairs={{0,24},{2,26},{4,28},{6,30},{8,16},{10,18},{12,20},{14,22},{16,8},... | collective-permute-start | bytes 442376 | tf_op jit(solution)/shard_map/ppermute | solution.py:778
  225.5 15.0 %collective-permute-start.25 = (bf16[48,1664]{1,0:T(8,128)(2,1)S(1)}, bf16[48,1664]{1,0:T(8,128)(2,1)S(1)}, u32[]{:S(2)}, u32[]{:S(2)}) collective-permute-start(bf16[48,1664]{1,0:T(8,128)(2,1)S(1)} %get-tuple-element.154), channel_id=1, source_target_pairs={{0,8},{2,10},{4,12},{6,14},{8,0},{10,2},{12,4},{14,6},{16,24},{18,... | collective-permute-start | bytes 479240 | tf_op jit(solution)/shard_map/ppermute | solution.py:778
  227.0 14.8 %collective-permute-start.26 = (bf16[48,1664]{1,0:T(8,128)(2,1)S(1)}, bf16[48,1664]{1,0:T(8,128)(2,1)S(1)}, u32[]{:S(2)}, u32[]{:S(2)}) collective-permute-start(bf16[48,1664]{1,0:T(8,128)(2,1)S(1)} %get-tuple-element.153), channel_id=1, source_target_pairs={{0,16},{2,18},{4,20},{6,22},{8,24},{10,26},{12,28},{14,30},{16,0},... | collective-permute-start | bytes 479240 | tf_op jit(solution)/shard_map/ppermute | solution.py:778
  237.6 10.8 %collective-permute-start.31 = (bf16[192,768]{1,0:T(8,128)(2,1)S(1)}, bf16[192,768]{1,0:T(8,128)(2,1)S(1)}, u32[]{:S(2)}, u32[]{:S(2)}) collective-permute-start(bf16[192,768]{1,0:T(8,128)(2,1)S(1)} %pad_maximum_fusion.3.refs_0_), channel_id=1, source_target_pairs={{0,4},{2,6},{4,0},{6,2},{8,12},{10,14},{12,8},{14,10},{16,20},{18,... | collective-permute-start | bytes 884744 | tf_op jit(solution)/shard_map/ppermute | solution.py:778
  248.6 12.8 %collective-permute-start.36 = (bf16[48,1664]{1,0:T(8,128)(2,1)S(1)}, bf16[48,1664]{1,0:T(8,128)(2,1)S(1)}, u32[]{:S(2)}, u32[]{:S(2)}) collective-permute-start(bf16[48,1664]{1,0:T(8,128)(2,1)S(1)} %fusion.7), channel_id=1, source_target_pairs={{0,16},{2,18},{4,20},{6,22},{8,24},{10,26},{12,28},{14,30},{16,0},... | collective-permute-start | bytes 479240 | tf_op jit(solution)/shard_map/ppermute | solution.py:778
  255.6 12.5 %collective-permute-start.40 = (bf16[192,768]{1,0:T(8,128)(2,1)S(1)}, bf16[192,768]{1,0:T(8,128)(2,1)S(1)}, u32[]{:S(2)}, u32[]{:S(2)}) collective-permute-start(bf16[192,768]{1,0:T(8,128)(2,1)S(1)} %collective-permute-done.31.refs_1_), channel_id=1, source_target_pairs={{0,2},{2,0},{4,6},{6,4},{8,10},{10,8},{12,14},{14,12},{16,18},{18,... | collective-permute-start | bytes 884744 | tf_op jit(solution)/shard_map/ppermute | solution.py:778
  264.1 11.3 %collective-permute-start.39 = (bf16[192,896]{1,0:T(8,128)(2,1)S(1)}, bf16[192,896]{1,0:T(8,128)(2,1)S(1)}, u32[]{:S(2)}, u32[]{:S(2)}) collective-permute-start(bf16[192,896]{1,0:T(8,128)(2,1)S(1)} %pad_maximum_fusion.2.refs_4_), channel_id=1, source_target_pairs={{0,2},{2,0},{4,6},{6,4},{8,10},{10,8},{12,14},{14,12},{16,18},{18,... | collective-permute-start | bytes 1032200 | tf_op jit(solution)/shard_map/ppermute | solution.py:778
  266.9 16.5 %collective-permute-start.44 = (bf16[192,896]{1,0:T(8,128)(2,1)S(1)}, bf16[192,896]{1,0:T(8,128)(2,1)S(1)}, u32[]{:S(2)}, u32[]{:S(2)}) collective-permute-start(bf16[192,896]{1,0:T(8,128)(2,1)S(1)} %pad_maximum_fusion.2.refs_4_), channel_id=1, source_target_pairs={{0,4},{2,6},{4,0},{6,2},{8,12},{10,14},{12,8},{14,10},{16,20},{18,... | collective-permute-start | bytes 1032200 | tf_op jit(solution)/shard_map/ppermute | solution.py:778
  275.4 11.2 %collective-permute-start.45 = (bf16[192,896]{1,0:T(8,128)(2,1)S(1)}, bf16[192,896]{1,0:T(8,128)(2,1)S(1)}, u32[]{:S(2)}, u32[]{:S(2)}) collective-permute-start(bf16[192,896]{1,0:T(8,128)(2,1)S(1)} %collective-permute-done.39.refs_5_), channel_id=1, source_target_pairs={{0,4},{2,6},{4,0},{6,2},{8,12},{10,14},{12,8},{14,10},{16,20},{18,... | collective-permute-start | bytes 1032200 | tf_op jit(solution)/shard_map/ppermute | solution.py:778
  (46 other events, 326.5 us)
Sparse Core Ops, SparseCore 0:
  28.8 78.8 all-gather.1
where the time goes:
time: 302 us; the launch traced here: 297 us
  Pallas kernels  148 us (49%)
  starting transfers between devices  54.2 us (18%)
  waiting for transfers between devices  53 us (18%)
  between operations  14.9 us (5%)
  local copies, waits for them, and re-layouts  11 us (4%)
  matrix products  8.44 us (3%)
  other arithmetic  7.33 us (2%)
    pallas_call x1, Pallas kernels, image_tower(): pl.pallas_call(tower_kernel, out_shape=jax.ShapeDtypeStruct((number, D),...  86.3 us
    ppermute x46, starting transfers between devices, swap(): lax.ppermute(values, axis, [(place, place ^ bit) for place in range(size)])  54.1 us
    ppermute x46, waiting for transfers between devices, swap(): lax.ppermute(values, axis, [(place, place ^ bit) for place in range(size)])  52.9 us
    pallas_call x1, Pallas kernels, text_forward(): pl.pallas_call(forward_kernel, out_shape=[shape((rows, 3 * D), bf16), sha...  17.2 us
    pallas_call x1, Pallas kernels, rest_backward(): pl.pallas_call(rest_kernel, out_shape=[shape((rows, D), f32), shape((D, B...  14.5 us
    pallas_call x1, Pallas kernels, loss_whole(): pl.pallas_call(loss_kernel, out_shape=[shape((number, 128), f32), shape((...  11.7 us
    dot_general x1, matrix products, dot_tn(): lax.dot_general(left_side, right_side, (((0,), (0,)), ((), ())), preferre...  8.44 us
    unnamed x52, local copies, waits for them, and re-layouts  8.15 us
  transfers between devices with their start and end apart: 47, of which 19 were waited for; matrix products, arithmetic and copies ran while one was open for 6% of the time, Pallas kernels for 43%

commit v1 on v0

--- a/solution.py
+++ b/solution.py
@@ -1186,8 +1186,9 @@
     up_column = behind(up_column, rest_sent)
     up_mine = spread_second(up_column, ups)
     up_near, up_across = spread_swaps(up_mine, ups, 2), spread_swaps(up_mine, ups, 1)
-    rest_came = behind(rest_came, up_near + up_across)
+    rest_came = behind(rest_came, up_mine)
     rest_chunk = reduce_last(rest_came, rest_kept)
+    (rest_chunk,) = behind([rest_chunk], up_near + up_across)
     rest_column = spread_first(rest_chunk)
     up_near = behind(up_near, [rest_chunk])
     up_last = spread_swaps(up_near, ups, 1)

time: 302 us -> 310 us (1.026)
  Pallas kernels: 148 us -> 118 us
  starting transfers between devices: 54.2 us -> 80.7 us
  waiting for transfers between devices: 53 us -> 65.9 us
    pallas_call x1, Pallas kernels: 86.3 us -> 56 us  [image_tower(): pl.pallas_call(tower_kernel, out_shape=jax.ShapeDtypeStruct((number, D),...]
    ppermute x46, starting transfers between devices: 54.1 us -> 80.6 us  [swap(): lax.ppermute(values, axis, [(place, place ^ bit) for place in range(size)])]
    ppermute x46, waiting for transfers between devices: 52.9 us -> 65.9 us  [swap(): lax.ppermute(values, axis, [(place, place ^ bit) for place in range(size)])]
  transfers between devices with their start and end apart: 47 -> 47, of which waited for: 19 -> 22; matrix products, arithmetic and copies ran while one was open for 6% -> 6% of each run, Pallas kernels for 43% -> 31%
where the time goes in v1:
time: 310 us; the launch traced here: 306 us
  Pallas kernels  118 us (38%)
  starting transfers between devices  80.7 us (26%)
  waiting for transfers between devices  65.9 us (21%)
  between operations  14.8 us (5%)
  local copies, waits for them, and re-layouts  11.4 us (4%)
  matrix products  8.44 us (3%)
  other arithmetic  7.34 us (2%)
    ppermute x46, starting transfers between devices, swap(): lax.ppermute(values, axis, [(place, place ^ bit) for place in range(size)])  80.6 us
    ppermute x46, waiting for transfers between devices, swap(): lax.ppermute(values, axis, [(place, place ^ bit) for place in range(size)])  65.9 us
    pallas_call x1, Pallas kernels, image_tower(): pl.pallas_call(tower_kernel, out_shape=jax.ShapeDtypeStruct((number, D),...  56 us
    pallas_call x1, Pallas kernels, text_forward(): pl.pallas_call(forward_kernel, out_shape=[shape((rows, 3 * D), bf16), sha...  17.2 us
    pallas_call x1, Pallas kernels, rest_backward(): pl.pallas_call(rest_kernel, out_shape=[shape((rows, D), f32), shape((D, B...  14.4 us
    pallas_call x1, Pallas kernels, loss_whole(): pl.pallas_call(loss_kernel, out_shape=[shape((number, 128), f32), shape((...  11.7 us
    unnamed x52, local copies, waits for them, and re-layouts  8.62 us
    dot_general x1, matrix products, dot_tn(): lax.dot_general(left_side, right_side, (((0,), (0,)), ((), ())), preferre...  8.44 us
  transfers between devices with their start and end apart: 47, of which 22 were waited for; matrix products, arithmetic and copies ran while one was open for 6% of the time, Pallas kernels for 31%

profile of v1, /device:TPU:8, one launch (start us, length us, event | category | flops | bytes accessed | tf_op | source)
XLA Modules:
  0.0 306.4 jit_solution(883048947817268779)
XLA Ops:
  10.6 17.2 %text_forward.1 = (bf16[512,2304]{1,0:T(8,128)(2,1)}, bf16[512,768]{1,0:T(8,128)(2,1)}, f32[512,768]{1,0:T(8,128)}, bf16[512,768]{1,0:T(8,128)(2,1)}, bf16[512,3...) custom-call(s32[32]{0:T(128)} %lens_ref.5, bf16[512,768]{1,0:T(8,128)(2,1)} %bitcast.11, ...), custom_call_target="tpu_custom_call" | custom-call | flops 7247757312 | bytes 25165824 | tf_op jit(solution)/shard_map/text_forward/pallas_call | solution.py:508
  29.8 56.0 %image_tower.1 = bf16[32,768]{1,0:T(8,128)(2,1)} custom-call(s32[32]{0:T(128)} %groups_ref.1, s32[1]{0:T(128)} %bitcast.1.mine_ref, bf16[145,32,768]{2,1,0:T(8,128)(2,1)} %bitcast.13, bf16[1,3072]{1,0:T(2,128)(2,1)} %copy-done.17, bf16[1,3072]{1,0:T(2,128)(2,1)} %copy-done.20, bf16[384,2304]{1,0:T(8,128)(2,1)} %qkv_own, bf16[384,2304]{1,0:T(8,128)(2,1)} %copy-done.18, ...), custom_call_target="tpu_custom_call" | custom-call | flops 30198988800 | bytes 25165824 | tf_op jit(solution)/shard_map/image_tower/pallas_call | solution.py:360
  85.8 11.6 %collective-permute-start.5 = (bf16[32,768]{1,0:T(8,128)(2,1)}, bf16[32,768]{1,0:T(8,128)(2,1)S(1)}, u32[]{:S(2)}, u32[]{:S(2)}) collective-permute-start(bf16[32,768]{1,0:T(8,128)(2,1)} %image_tower.1), channel_id=1, source_target_pairs={{0,8},{2,10},{4,12},{6,14},{8,0},{10,2},{12,4},{14,6},{16,24},{18,... | collective-permute-start | bytes 147464 | tf_op jit(solution)/shard_map/ppermute | solution.py:778
  97.5 3.2 %collective-permute-start.6 = (bf16[32,768]{1,0:T(8,128)(2,1)}, bf16[32,768]{1,0:T(8,128)(2,1)S(1)}, u32[]{:S(2)}, u32[]{:S(2)}) collective-permute-start(bf16[32,768]{1,0:T(8,128)(2,1)} %image_tower.1), channel_id=1, source_target_pairs={{0,16},{2,18},{4,20},{6,22},{8,24},{10,26},{12,28},{14,30},{16,0},... | collective-permute-start | bytes 147464 | tf_op jit(solution)/shard_map/ppermute | solution.py:778
  102.0 3.4 %collective-permute-done.6 = bf16[32,768]{1,0:T(8,128)(2,1)S(1)} collective-permute-done((bf16[32,768]{1,0:T(8,128)(2,1)}, bf16[32,768]{1,0:T(8,128)(2,1)S(1)}, u32[]{:S(2)}, u32[]{:S(2)}) %collective-permute-start.6) | collective-permute-done | bytes 49184 | tf_op jit(solution)/shard_map/ppermute | solution.py:778
  106.6 18.9 %collective-permute-start.8 = (bf16[128,768]{1,0:T(8,128)(2,1)S(1)}, bf16[128,768]{1,0:T(8,128)(2,1)S(1)}, u32[]{:S(2)}, u32[]{:S(2)}) collective-permute-start(bf16[128,768]{1,0:T(8,128)(2,1)S(1)} %pad_maximum_fusion.6), channel_id=1, source_target_pairs={{0,2},{2,0},{4,6},{6,4},{8,10},{10,8},{12,14},{14,12},{16,18},{18,... | collective-permute-start | bytes 589832 | tf_op jit(solution)/shard_map/ppermute | solution.py:778
  125.5 7.6 %collective-permute-start.9 = (bf16[128,768]{1,0:T(8,128)(2,1)S(1)}, bf16[128,768]{1,0:T(8,128)(2,1)S(1)}, u32[]{:S(2)}, u32[]{:S(2)}) collective-permute-start(bf16[128,768]{1,0:T(8,128)(2,1)S(1)} %pad_maximum_fusion.6), channel_id=1, source_target_pairs={{0,4},{2,6},{4,0},{6,2},{8,12},{10,14},{12,8},{14,10},{16,20},{18,... | collective-permute-start | bytes 589832 | tf_op jit(solution)/shard_map/ppermute | solution.py:778
  133.2 5.2 %collective-permute-done.9 = bf16[128,768]{1,0:T(8,128)(2,1)S(1)} collective-permute-done((bf16[128,768]{1,0:T(8,128)(2,1)S(1)}, bf16[128,768]{1,0:T(8,128)(2,1)S(1)}, u32[]{:S(2)}, u32[]{:S(2)}) %collective-permute-start.9) | collective-permute-done | bytes 196640 | tf_op jit(solution)/shard_map/ppermute | solution.py:778
  144.0 11.7 %pair_loss.1 = (f32[32,128]{1,0:T(8,128)S(1)}, f32[32,768]{1,0:T(8,128)S(1)}, bf16[32,768]{1,0:T(8,128)(2,1)S(1)}, bf16[1024,768]{1,0:T(8,128)(2,1)S(1)}) custom-call(s32[2]{0:T(128)S(1)} %pad_add_fusion.1.where_ref, bf16[1024,896]{1,0:T(8,128)(2,1)S(1)} %slice.214.early_ref, bf16[1024,768]{1,0:T(8,128)(2,1)S(1)} %constant_dynamic-update-slice_fusion.7.image_ref, ...), custom_call_target="tpu_custom_call" | custom-call | tf_op jit(solution)/shard_map/pair_loss/pallas_call | solution.py:1025
  159.9 6.5 %up_backward.1 = (bf16[512,3072]{1,0:T(8,128)(2,1)S(1)}, f32[768,1536]{1,0:T(8,128)S(1)}, bf16[768,1536]{1,0:T(8,128)(2,1)S(1)}, f32[1,3072]{1,0:T(1,128)S(1)}) custom-call(s32[2,16]{1,0:T(2,128)S(1)} %pad_add_fusion.place_ref, s32[1]{0:T(128)} %bitcast.1.mine_ref, s32[32]{0:T(128)S(1)} %copy-done.8, bf16[32,768]{1,0:T(8,128)(2,1)S(1)} %get-tuple-element.95.branch_ref, ...), custom_call_target="tpu_custom_call" | custom-call | flops 2415919104 | bytes 20971520 | tf_op jit(solution)/shard_map/up_backward/pallas_call | solution.py:571
  166.7 5.6 %mlp_backward.1 = (f32[512,768]{1,0:T(8,128)S(1)}, bf16[512,768]{1,0:T(8,128)(2,1)S(1)}, f32[1,768]{1,0:T(1,128)S(1)}) custom-call(s32[32]{0:T(128)S(1)} %copy-done.8, bf16[512,3072]{1,0:T(8,128)(2,1)S(1)} %get-tuple-element.98.pre_ref, f32[32,768]{1,0:T(8,128)S(1)} %get-tuple-element.99.grad_ref, f32[512,768]{1,0:T(8,128)S(1)} %copy-done.11, ...), custom_call_target="tpu_custom_call" | custom-call | flops 3019898880 | bytes 20971520 | tf_op jit(solution)/shard_map/mlp_backward/pallas_call | solution.py:613
  175.5 14.4 %rest_backward.1 = (f32[512,768]{1,0:T(8,128)}, f32[768,1664]{1,0:T(8,128)}, bf16[768,1664]{1,0:T(8,128)(2,1)}) custom-call(s32[2,16]{1,0:T(2,128)S(1)} %pad_add_fusion.place_ref, s32[1]{0:T(128)} %bitcast.1.mine_ref, bf16[512,2304]{1,0:T(8,128)(2,1)S(1)} %copy-done.12, bf16[6144,128]{1,0:T(8,128)(2,1)S(1)} %copy-done.13, bf16[512,768]{1,0:T(8,128)(2,1)S(1)} %copy-done.14, ...), custom_call_target="tpu_custom_call" | custom-call | flops 28991029248 | bytes 62914560 | tf_op jit(solution)/shard_map/rest_backward/pallas_call | solution.py:742
  197.9 5.2 %collective-permute-done.18 = bf16[192,768]{1,0:T(8,128)(2,1)S(1)} collective-permute-done((bf16[192,768]{1,0:T(8,128)(2,1)S(1)}, bf16[192,768]{1,0:T(8,128)(2,1)S(1)}, u32[]{:S(2)}, u32[]{:S(2)}) %collective-permute-start.18) | collective-permute-done | bytes 294944 | tf_op jit(solution)/shard_map/ppermute | solution.py:778
  204.7 3.8 %collective-permute-start.22 = (bf16[48,1536]{1,0:T(8,128)(2,1)S(1)}, bf16[48,1536]{1,0:T(8,128)(2,1)S(1)}, u32[]{:S(2)}, u32[]{:S(2)}) collective-permute-start(bf16[48,1536]{1,0:T(8,128)(2,1)S(1)} %get-tuple-element.159), channel_id=1, source_target_pairs={{0,8},{2,10},{4,12},{6,14},{8,0},{10,2},{12,4},{14,6},{16,24},{18,... | collective-permute-start | bytes 442376 | tf_op jit(solution)/shard_map/ppermute | solution.py:778
  210.0 8.4 %fusion = f32[3072,384]{1,0:T(8,128)} fusion(bf16[1024,3968]{1,0:T(8,128)(2,1)} %all-gather.2.cloned.1.call-done, bf16[1024,768]{1,0:T(8,128)(2,1)S(1)} %copy-done.5, s32[]{:T(128)S(6)} %select_n.77), kind=kOutput, calls=%fused_computation | convolution fusion | flops 2415919104 | bytes 11796484 | tf_op jit(solution)/shard_map/dot_general | solution.py:48
  228.1 3.8 %collective-permute-start.25 = (bf16[48,1664]{1,0:T(8,128)(2,1)S(1)}, bf16[48,1664]{1,0:T(8,128)(2,1)S(1)}, u32[]{:S(2)}, u32[]{:S(2)}) collective-permute-start(bf16[48,1664]{1,0:T(8,128)(2,1)S(1)} %get-tuple-element.156), channel_id=1, source_target_pairs={{0,8},{2,10},{4,12},{6,14},{8,0},{10,2},{12,4},{14,6},{16,24},{18,... | collective-permute-start | bytes 479240 | tf_op jit(solution)/shard_map/ppermute | solution.py:778
  234.3 11.7 %collective-permute-done.30 = bf16[48,1536]{1,0:T(8,128)(2,1)S(1)} collective-permute-done((bf16[48,1536]{1,0:T(8,128)(2,1)S(1)}, bf16[48,1536]{1,0:T(8,128)(2,1)S(1)}, u32[]{:S(2)}, u32[]{:S(2)}) %collective-permute-start.30) | collective-permute-done | bytes 147488 | tf_op jit(solution)/shard_map/ppermute | solution.py:778
  251.7 4.2 %collective-permute-done.31.refs_1_ = bf16[192,768]{1,0:T(8,128)(2,1)S(1)} collective-permute-done((bf16[192,768]{1,0:T(8,128)(2,1)S(1)}, bf16[192,768]{1,0:T(8,128)(2,1)S(1)}, u32[]{:S(2)}, u32[]{:S(2)}) %collective-permute-start.31) | collective-permute-done | bytes 294944 | tf_op jit(solution)/shard_map/ppermute | solution.py:778
  255.9 4.0 %collective-permute-done.32.refs_5_ = bf16[192,768]{1,0:T(8,128)(2,1)S(1)} collective-permute-done((bf16[192,768]{1,0:T(8,128)(2,1)S(1)}, bf16[192,768]{1,0:T(8,128)(2,1)S(1)}, u32[]{:S(2)}, u32[]{:S(2)}) %collective-permute-start.32) | collective-permute-done | bytes 294944 | tf_op jit(solution)/shard_map/ppermute | solution.py:778
  265.9 3.8 %collective-permute-done.36 = bf16[48,1664]{1,0:T(8,128)(2,1)S(1)} collective-permute-done((bf16[48,1664]{1,0:T(8,128)(2,1)S(1)}, bf16[48,1664]{1,0:T(8,128)(2,1)S(1)}, u32[]{:S(2)}, u32[]{:S(2)}) %collective-permute-start.36) | collective-permute-done | bytes 159776 | tf_op jit(solution)/shard_map/ppermute | solution.py:778
  269.7 4.0 %collective-permute-done.37 = bf16[48,1664]{1,0:T(8,128)(2,1)S(1)} collective-permute-done((bf16[48,1664]{1,0:T(8,128)(2,1)S(1)}, bf16[48,1664]{1,0:T(8,128)(2,1)S(1)}, u32[]{:S(2)}, u32[]{:S(2)}) %collective-permute-start.37) | collective-permute-done | bytes 159776 | tf_op jit(solution)/shard_map/ppermute | solution.py:778
  279.1 4.8 %collective-permute-done.38.refs_1_ = bf16[192,768]{1,0:T(8,128)(2,1)S(1)} collective-permute-done((bf16[192,768]{1,0:T(8,128)(2,1)S(1)}, bf16[192,768]{1,0:T(8,128)(2,1)S(1)}, u32[]{:S(2)}, u32[]{:S(2)}) %collective-permute-start.38) | collective-permute-done | bytes 294944 | tf_op jit(solution)/shard_map/ppermute | solution.py:778
  287.5 5.2 %collective-permute-done.42.refs_2_ = bf16[192,768]{1,0:T(8,128)(2,1)S(1)} collective-permute-done((bf16[192,768]{1,0:T(8,128)(2,1)S(1)}, bf16[192,768]{1,0:T(8,128)(2,1)S(1)}, u32[]{:S(2)}, u32[]{:S(2)}) %collective-permute-start.42) | collective-permute-done | bytes 294944 | tf_op jit(solution)/shard_map/ppermute | solution.py:778
  292.7 3.2 %collective-permute-done.43.refs_3_ = bf16[192,768]{1,0:T(8,128)(2,1)S(1)} collective-permute-done((bf16[192,768]{1,0:T(8,128)(2,1)S(1)}, bf16[192,768]{1,0:T(8,128)(2,1)S(1)}, u32[]{:S(2)}, u32[]{:S(2)}) %collective-permute-start.43) | collective-permute-done | bytes 294944 | tf_op jit(solution)/shard_map/ppermute | solution.py:778
  (181 shorter events, 68.0 us)
Async XLA Ops:
  7.2 135.0 %all-gather.2.cloned.1.call-start = ((), (), s32[]{:S(2)}) async-start(), calls=%async_computation | async-start | bytes 8380416 | tf_op jit(solution)/shard_map/all_gather | solution.py:1113
  7.2 21.4 %collective-permute-start.3 = (bf16[384,3072]{1,0:T(8,128)(2,1)}, bf16[384,3072]{1,0:T(8,128)(2,1)}, u32[]{:S(2)}, u32[]{:S(2)}) collective-permute-start(bf16[384,3072]{1,0:T(8,128)(2,1)} %up_own), channel_id=1, source_target_pairs={{0,1},{1,0},{2,3},{3,2},{4,5},{5,4},{6,7},{7,6},{8,9},{9,8},{10,11... | collective-permute-start | bytes 7077896 | tf_op jit(solution)/shard_map/ppermute | solution.py:778
  7.3 21.3 %collective-permute-start.4 = (bf16[1536,768]{1,0:T(8,128)(2,1)}, bf16[1536,768]{1,0:T(8,128)(2,1)}, u32[]{:S(2)}, u32[]{:S(2)}) collective-permute-start(bf16[1536,768]{1,0:T(8,128)(2,1)} %down_own), channel_id=1, source_target_pairs={{0,1},{1,0},{2,3},{3,2},{4,5},{5,4},{6,7},{7,6},{8,9},{9,8},{10,11... | collective-permute-start | bytes 7077896 | tf_op jit(solution)/shard_map/ppermute | solution.py:778
  7.8 20.0 %collective-permute-start.1 = (bf16[384,2304]{1,0:T(8,128)(2,1)}, bf16[384,2304]{1,0:T(8,128)(2,1)S(1)}, u32[]{:S(2)}, u32[]{:S(2)}) collective-permute-start(bf16[384,2304]{1,0:T(8,128)(2,1)} %qkv_own), channel_id=1, source_target_pairs={{0,1},{1,0},{2,3},{3,2},{4,5},{5,4},{6,7},{7,6},{8,9},{9,8},{10,11... | collective-permute-start | bytes 5308424 | tf_op jit(solution)/shard_map/ppermute | solution.py:778
  8.6 19.1 %collective-permute-start = (bf16[1,3072]{1,0:T(2,128)(2,1)S(1)}, bf16[1,3072]{1,0:T(2,128)(2,1)S(1)}, u32[]{:S(2)}, u32[]{:S(2)}) collective-permute-start(bf16[1,3072]{1,0:T(2,128)(2,1)S(1)} %broadcast_in_dim.11.vec_own_ref), channel_id=1, source_target_pairs={{0,1},{1,0},{2,3},{3,2},{4,5},{5,4},{6,7},{7,6},{8,9},{9,8},{10,11... | collective-permute-start | bytes 18440 | tf_op jit(solution)/shard_map/ppermute | solution.py:778
  9.1 18.6 %collective-permute-start.2 = (bf16[384,768]{1,0:T(8,128)(2,1)}, bf16[384,768]{1,0:T(8,128)(2,1)S(1)}, u32[]{:S(2)}, u32[]{:S(2)}) collective-permute-start(bf16[384,768]{1,0:T(8,128)(2,1)} %out_own), channel_id=1, source_target_pairs={{0,1},{1,0},{2,3},{3,2},{4,5},{5,4},{6,7},{7,6},{8,9},{9,8},{10,11... | collective-permute-start | bytes 1769480 | tf_op jit(solution)/shard_map/ppermute | solution.py:778
  85.8 16.2 %collective-permute-start.5 = (bf16[32,768]{1,0:T(8,128)(2,1)}, bf16[32,768]{1,0:T(8,128)(2,1)S(1)}, u32[]{:S(2)}, u32[]{:S(2)}) collective-permute-start(bf16[32,768]{1,0:T(8,128)(2,1)} %image_tower.1), channel_id=1, source_target_pairs={{0,8},{2,10},{4,12},{6,14},{8,0},{10,2},{12,4},{14,6},{16,24},{18,... | collective-permute-start | bytes 147464 | tf_op jit(solution)/shard_map/ppermute | solution.py:778
  106.6 26.6 %collective-permute-start.8 = (bf16[128,768]{1,0:T(8,128)(2,1)S(1)}, bf16[128,768]{1,0:T(8,128)(2,1)S(1)}, u32[]{:S(2)}, u32[]{:S(2)}) collective-permute-start(bf16[128,768]{1,0:T(8,128)(2,1)S(1)} %pad_maximum_fusion.6), channel_id=1, source_target_pairs={{0,2},{2,0},{4,6},{6,4},{8,10},{10,8},{12,14},{14,12},{16,18},{18,... | collective-permute-start | bytes 589832 | tf_op jit(solution)/shard_map/ppermute | solution.py:778
  125.5 12.9 %collective-permute-start.9 = (bf16[128,768]{1,0:T(8,128)(2,1)S(1)}, bf16[128,768]{1,0:T(8,128)(2,1)S(1)}, u32[]{:S(2)}, u32[]{:S(2)}) collective-permute-start(bf16[128,768]{1,0:T(8,128)(2,1)S(1)} %pad_maximum_fusion.6), channel_id=1, source_target_pairs={{0,4},{2,6},{4,0},{6,2},{8,12},{10,14},{12,8},{14,10},{16,20},{18,... | collective-permute-start | bytes 589832 | tf_op jit(solution)/shard_map/ppermute | solution.py:778
  173.7 16.3 %collective-permute-start.13 = (bf16[384,768]{1,0:T(8,128)(2,1)S(1)}, bf16[384,768]{1,0:T(8,128)(2,1)S(1)}, u32[]{:S(2)}, u32[]{:S(2)}) collective-permute-start(bf16[384,768]{1,0:T(8,128)(2,1)S(1)} %get-tuple-element.153), channel_id=1, source_target_pairs={{0,2},{2,0},{4,6},{6,4},{8,10},{10,8},{12,14},{14,12},{16,18},{18,... | collective-permute-start | bytes 1769480 | tf_op jit(solution)/shard_map/ppermute | solution.py:778
  174.3 15.6 %collective-permute-start.14 = (bf16[384,768]{1,0:T(8,128)(2,1)S(1)}, bf16[384,768]{1,0:T(8,128)(2,1)}, u32[]{:S(2)}, u32[]{:S(2)}) collective-permute-start(bf16[384,768]{1,0:T(8,128)(2,1)S(1)} %get-tuple-element.152), channel_id=1, source_target_pairs={{0,4},{2,6},{4,0},{6,2},{8,12},{10,14},{12,8},{14,10},{16,20},{18,... | collective-permute-start | bytes 1769480 | tf_op jit(solution)/shard_map/ppermute | solution.py:778
  195.4 23.0 %collective-permute-start.16 = (bf16[384,768]{1,0:T(8,128)(2,1)S(1)}, bf16[384,768]{1,0:T(8,128)(2,1)S(1)}, u32[]{:S(2)}, u32[]{:S(2)}) collective-permute-start(bf16[384,768]{1,0:T(8,128)(2,1)S(1)} %add_convert_fusion.1), channel_id=1, source_target_pairs={{0,2},{2,0},{4,6},{6,4},{8,10},{10,8},{12,14},{14,12},{16,18},{18,... | collective-permute-start | bytes 1769480 | tf_op jit(solution)/shard_map/ppermute | solution.py:778
  196.9 21.5 %collective-permute-start.17 = (bf16[384,896]{1,0:T(8,128)(2,1)S(1)}, bf16[384,896]{1,0:T(8,128)(2,1)S(1)}, u32[]{:S(2)}, u32[]{:S(2)}) collective-permute-start(bf16[384,896]{1,0:T(8,128)(2,1)S(1)} %add_convert_fusion), channel_id=1, source_target_pairs={{0,4},{2,6},{4,0},{6,2},{8,12},{10,14},{12,8},{14,10},{16,20},{18,... | collective-permute-start | bytes 2064392 | tf_op jit(solution)/shard_map/ppermute | solution.py:778
  204.7 16.3 %collective-permute-start.22 = (bf16[48,1536]{1,0:T(8,128)(2,1)S(1)}, bf16[48,1536]{1,0:T(8,128)(2,1)S(1)}, u32[]{:S(2)}, u32[]{:S(2)}) collective-permute-start(bf16[48,1536]{1,0:T(8,128)(2,1)S(1)} %get-tuple-element.159), channel_id=1, source_target_pairs={{0,8},{2,10},{4,12},{6,14},{8,0},{10,2},{12,4},{14,6},{16,24},{18,... | collective-permute-start | bytes 442376 | tf_op jit(solution)/shard_map/ppermute | solution.py:778
  208.5 12.5 %collective-permute-start.23 = (bf16[48,1536]{1,0:T(8,128)(2,1)S(1)}, bf16[48,1536]{1,0:T(8,128)(2,1)S(1)}, u32[]{:S(2)}, u32[]{:S(2)}) collective-permute-start(bf16[48,1536]{1,0:T(8,128)(2,1)S(1)} %get-tuple-element.158), channel_id=1, source_target_pairs={{0,16},{2,18},{4,20},{6,22},{8,24},{10,26},{12,28},{14,30},{16,0},... | collective-permute-start | bytes 442376 | tf_op jit(solution)/shard_map/ppermute | solution.py:778
  208.5 12.6 %collective-permute-start.24 = (bf16[48,1536]{1,0:T(8,128)(2,1)S(1)}, bf16[48,1536]{1,0:T(8,128)(2,1)S(1)}, u32[]{:S(2)}, u32[]{:S(2)}) collective-permute-start(bf16[48,1536]{1,0:T(8,128)(2,1)S(1)} %get-tuple-element.157), channel_id=1, source_target_pairs={{0,24},{2,26},{4,28},{6,30},{8,16},{10,18},{12,20},{14,22},{16,8},... | collective-permute-start | bytes 442376 | tf_op jit(solution)/shard_map/ppermute | solution.py:778
  224.0 22.0 %collective-permute-start.30 = (bf16[48,1536]{1,0:T(8,128)(2,1)S(1)}, bf16[48,1536]{1,0:T(8,128)(2,1)S(1)}, u32[]{:S(2)}, u32[]{:S(2)}) collective-permute-start(bf16[48,1536]{1,0:T(8,128)(2,1)S(1)} %fusion.10), channel_id=1, source_target_pairs={{0,24},{2,26},{4,28},{6,30},{8,16},{10,18},{12,20},{14,22},{16,8},... | collective-permute-start | bytes 442376 | tf_op jit(solution)/shard_map/ppermute | solution.py:778
  228.1 20.1 %collective-permute-start.25 = (bf16[48,1664]{1,0:T(8,128)(2,1)S(1)}, bf16[48,1664]{1,0:T(8,128)(2,1)S(1)}, u32[]{:S(2)}, u32[]{:S(2)}) collective-permute-start(bf16[48,1664]{1,0:T(8,128)(2,1)S(1)} %get-tuple-element.156), channel_id=1, source_target_pairs={{0,8},{2,10},{4,12},{6,14},{8,0},{10,2},{12,4},{14,6},{16,24},{18,... | collective-permute-start | bytes 479240 | tf_op jit(solution)/shard_map/ppermute | solution.py:778
  232.0 17.4 %collective-permute-start.26 = (bf16[48,1664]{1,0:T(8,128)(2,1)S(1)}, bf16[48,1664]{1,0:T(8,128)(2,1)S(1)}, u32[]{:S(2)}, u32[]{:S(2)}) collective-permute-start(bf16[48,1664]{1,0:T(8,128)(2,1)S(1)} %get-tuple-element.155), channel_id=1, source_target_pairs={{0,16},{2,18},{4,20},{6,22},{8,24},{10,26},{12,28},{14,30},{16,0},... | collective-permute-start | bytes 479240 | tf_op jit(solution)/shard_map/ppermute | solution.py:778
  232.0 19.6 %collective-permute-start.27 = (bf16[48,1664]{1,0:T(8,128)(2,1)S(1)}, bf16[48,1664]{1,0:T(8,128)(2,1)S(1)}, u32[]{:S(2)}, u32[]{:S(2)}) collective-permute-start(bf16[48,1664]{1,0:T(8,128)(2,1)S(1)} %get-tuple-element.154), channel_id=1, source_target_pairs={{0,24},{2,26},{4,28},{6,30},{8,16},{10,18},{12,20},{14,22},{16,8},... | collective-permute-start | bytes 479240 | tf_op jit(solution)/shard_map/ppermute | solution.py:778
  247.3 12.6 %collective-permute-start.33 = (bf16[192,768]{1,0:T(8,128)(2,1)S(1)}, bf16[192,768]{1,0:T(8,128)(2,1)S(1)}, u32[]{:S(2)}, u32[]{:S(2)}) collective-permute-start(bf16[192,768]{1,0:T(8,128)(2,1)S(1)} %pad_maximum_fusion.3.refs_0_), channel_id=1, source_target_pairs={{0,2},{2,0},{4,6},{6,4},{8,10},{10,8},{12,14},{14,12},{16,18},{18,... | collective-permute-start | bytes 884744 | tf_op jit(solution)/shard_map/ppermute | solution.py:778
  260.8 12.9 %collective-permute-start.37 = (bf16[48,1664]{1,0:T(8,128)(2,1)S(1)}, bf16[48,1664]{1,0:T(8,128)(2,1)S(1)}, u32[]{:S(2)}, u32[]{:S(2)}) collective-permute-start(bf16[48,1664]{1,0:T(8,128)(2,1)S(1)} %fusion.7), channel_id=1, source_target_pairs={{0,24},{2,26},{4,28},{6,30},{8,16},{10,18},{12,20},{14,22},{16,8},... | collective-permute-start | bytes 479240 | tf_op jit(solution)/shard_map/ppermute | solution.py:778
  263.4 12.6 %collective-permute-start.40 = (bf16[192,768]{1,0:T(8,128)(2,1)S(1)}, bf16[192,768]{1,0:T(8,128)(2,1)S(1)}, u32[]{:S(2)}, u32[]{:S(2)}) collective-permute-start(bf16[192,768]{1,0:T(8,128)(2,1)S(1)} %collective-permute-done.31.refs_1_), channel_id=1, source_target_pairs={{0,2},{2,0},{4,6},{6,4},{8,10},{10,8},{12,14},{14,12},{16,18},{18,... | collective-permute-start | bytes 884744 | tf_op jit(solution)/shard_map/ppermute | solution.py:778
  274.9 17.8 %collective-permute-start.44 = (bf16[192,896]{1,0:T(8,128)(2,1)S(1)}, bf16[192,896]{1,0:T(8,128)(2,1)S(1)}, u32[]{:S(2)}, u32[]{:S(2)}) collective-permute-start(bf16[192,896]{1,0:T(8,128)(2,1)S(1)} %pad_maximum_fusion.2.refs_4_), channel_id=1, source_target_pairs={{0,4},{2,6},{4,0},{6,2},{8,12},{10,14},{12,8},{14,10},{16,20},{18,... | collective-permute-start | bytes 1032200 | tf_op jit(solution)/shard_map/ppermute | solution.py:778
  (46 other events, 340.0 us)
Sparse Core Ops, SparseCore 0:
  28.8 78.8 all-gather.1
